TPU v7x, 32 devices: a whole 2x2x4 slice. The times are simulated.
32 devices in a mesh: wa: 4 (over y, core), row: 8 (over z, x).
Axes of the slice: x: 2, y: 2, z: 4, core: 2. Of those that a mesh axis runs over, the one named last changes fastest.
Arguments:
- activations: bfloat16 [24, 1280, 512], P('row', 'wa'), may hold values from -1300 to 1300, as said below
- gain_one: float32 [1280], P('wa'), may hold values from 0.1 to 1.9
- shift_one: float32 [1280], P('wa'), may hold values from -3 to 3
- kernel_one: bfloat16 [3, 3, 8, 4, 51200], P(None, None, 'row', 'wa'), may hold values from -0.0546875 to 0.0546875
- bias_one: float32 [1280], P('wa'), may hold values from -3 to 3
- gain_two: float32 [1280], P('wa'), may hold values from 0.1 to 1.9
- shift_two: float32 [1280], P('wa'), may hold values from -3 to 3
- kernel_two: bfloat16 [3, 3, 8, 4, 51200], P(None, None, 'row', 'wa'), may hold values from -0.0546875 to 0.0546875
- bias_two: float32 [1280], P('wa'), may hold values from -3 to 3
Outputs:
- result: bfloat16 [24, 1280, 512], P('row', 'wa')
Inputs may be any that keep to these rules, and one draw needn't show every extreme that they name: `activations`: real-valued feature maps whose magnitude differs from pixel row to pixel row, from pixel to pixel and from channel to channel.
All inputs are finite; a program needn't handle non-finite values.
Results may differ from a plain program's by a relative error of at most 0.0056.
Values may be sent and summed in bfloat16 or wider, within the bound.
No kernel may reach another device: no remote copies, remote signals or barrier semaphores. Data moves between devices by JAX's collectives and lax.ppermute only.
A program may use at most 128 MiB of HBM per device.

v0:
```python
import jax
import jax.numpy as jnp
from jax import lax
from jax.sharding import PartitionSpec as P

C = 1280
GROUPS = 32
WIDTH = 32


def padded_2(cells, sides, width):
    for axis, dim in sides:
        count = lax.axis_size(axis)
        ends = count - 1
        head = lax.slice_in_dim(cells, 0, width, axis=dim)
        tail = lax.slice_in_dim(cells, cells.shape[dim] - width, cells.shape[dim], axis=dim)
        cells = jnp.concatenate(
            [
                lax.ppermute(tail, axis, [(i, (i + 1) % count) for i in range(ends)]),
                cells,
                lax.ppermute(head, axis, [((i + 1) % count, i) for i in range(ends)]),
            ],
            axis=dim,
        )
    return cells


def activate(field, gain, shift):
    rows_here, local_chans, col_count = field.shape
    group_size = C // GROUPS
    image_count = col_count // WIDTH
    grouped = field.reshape(rows_here, local_chans // group_size, group_size, image_count, WIDTH)
    total_count = rows_here * lax.axis_size("row") * WIDTH * group_size
    center = lax.psum(jnp.sum(grouped, axis=(0, 2, 4)), "row") / total_count
    offset = grouped - center[None, :, None, :, None]
    spread = lax.psum(jnp.sum(jnp.square(offset), axis=(0, 2, 4)), "row") / total_count
    normed = (offset * lax.rsqrt(spread + 1e-05)[None, :, None, :, None]).reshape(field.shape)
    return jax.nn.silu(normed * gain[:, None] + shift[:, None]).astype(jnp.bfloat16)


def panel_of(shard):
    wide_rows = lax.all_gather(shard, "wa", axis=1, tiled=True)
    widened = padded_2(wide_rows, (("row", 0),), 1)
    return widened


def shift_columns(tap_sum, offset):
    col_count = tap_sum.shape[2]
    column_place = lax.broadcasted_iota(jnp.int32, (1, 1, col_count), 2) % WIDTH
    if offset < 0:
        displaced = jnp.pad(tap_sum[:, :, :-1], ((0, 0), (0, 0), (1, 0)))
        inside = column_place != 0
    else:
        displaced = jnp.pad(tap_sum[:, :, 1:], ((0, 0), (0, 0), (0, 1)))
        inside = column_place != WIDTH - 1
    return jnp.where(inside, displaced, 0.0)


def convolve(shard, kernel, bias):
    padded = panel_of(shard)
    rows_here = padded.shape[0] - 2
    col_count = padded.shape[2]
    out_chans = shard.shape[1]
    block_in = kernel.shape[4] // out_chans
    zeroed = jnp.zeros((rows_here, out_chans, col_count), jnp.float32)
    running = zeroed
    weights_piece = lax.all_gather(kernel, "row", axis=2, tiled=True)
    inner_count = weights_piece.shape[2] * block_in
    weight_slab = weights_piece.reshape(3, 3, inner_count, out_chans)
    for col_tap in range(3):
        tap_sum = jnp.zeros((rows_here, out_chans, col_count), jnp.float32)
        for row_tap in range(3):
            window = padded[row_tap : row_tap + rows_here]
            tap_sum = tap_sum + jnp.einsum(
                "rcw,co->row",
                window,
                weight_slab[row_tap, col_tap],
                preferred_element_type=jnp.float32,
            )
        if col_tap == 1:
            running = running + tap_sum
        else:
            running = running + shift_columns(tap_sum, col_tap - 1)
    return running + bias[None, :, None]


def per_device(
    activations,
    gain_one,
    shift_one,
    kernel_one,
    bias_one,
    gain_two,
    shift_two,
    kernel_two,
    bias_two,
):
    kernels = (kernel_one, kernel_two)
    first = activate(activations.astype(jnp.float32), gain_one, shift_one)
    hidden = convolve(first, kernels[0], bias_one).astype(jnp.bfloat16)
    second = activate(hidden.astype(jnp.float32), gain_two, shift_two)
    return convolve(second, kernels[1], bias_two).astype(jnp.bfloat16)


def solution(mesh):
    placed = (
        P("row", "wa", None),
        P("wa"),
        P("wa"),
        P(None, None, "row", "wa", None),
        P("wa"),
        P("wa"),
        P("wa"),
        P(None, None, "row", "wa", None),
        P("wa"),
    )
    return jax.shard_map(
        per_device, mesh=mesh, in_specs=placed, out_specs=P("row", "wa", None), check_vma=False
    )
```

profile of v0, /device:TPU:0, one launch (start us, length us, event | category | flops | bytes accessed | tf_op | source)
XLA Modules:
  0.0 526.6 jit_solution(320209838201149113)
XLA Ops:
  6.5 1.4 convert_reduce_fusion.1
  8.0 0.3 copy.34
  8.2 0.8 reduce_sum.47
  9.3 23.5 %psum.28 = f32[8,16]{0,1:T(8,128)S(1)} all-reduce(f32[8,16]{0,1:T(8,128)S(1)} %reduce_sum.51), channel_id=1, replica_groups=mesh['wa'=4,'row'=8] {'row'}, use_global_device_ids=true, to_apply=%region_2.0 | all-reduce | flops 128 | bytes 1024 | tf_op jit(solution)/shard_map/psum | solution.py:34
  33.0 1.5 sub.29
  34.5 1.4 copy.35
  35.9 0.3 fusion.13
  36.2 0.6 copy-done.2
  36.7 1.1 copy.36
  37.9 1.9 reduce_sum.53
  40.0 17.4 %psum.29 = f32[8,16]{0,1:T(8,128)S(1)} all-reduce(f32[8,16]{0,1:T(8,128)S(1)} %reduce_sum.54), channel_id=1, replica_groups=mesh['wa'=4,'row'=8] {'row'}, use_global_device_ids=true, to_apply=%region_5.6 | all-reduce | flops 128 | bytes 1024 | tf_op jit(solution)/shard_map/psum | solution.py:36
  57.6 1.5 mul.50
  59.1 1.4 copy.37
  60.5 2.8 fusion.21
  63.4 0.7 all-gather.7.cloned.1.call-update
  64.1 0.7 all-gather.11.cloned.1.call-update
  64.9 30.3 %all-gather.5.cloned.1.call-done = bf16[3,1280,512]{2,1,0:T(8,128)(2,1)} async-done(((bf16[3,320,512]{2,1,0:T(8,128)(2,1)}), bf16[3,1280,512]{2,1,0:T(8,128)(2,1)}) %all-gather.5.cloned.1.call-update) | async-done | bytes 3932176 | tf_op jit(solution)/shard_map/all_gather | solution.py:42
  95.2 1.9 fusion.52
  97.1 4.4 collective-permute-start
  101.5 1.3 collective-permute-start.1
  102.8 166.5 %all-gather.7.cloned.1.call-done = bf16[3,3,8,1,51200]{4,1,3,2,0:T(4,128)(2,1)} async-done(((bf16[3,3,1,1,51200]{4,1,3,2,0:T(4,128)(2,1)}), bf16[3,3,8,1,51200]{4,1,3,2,0:T(4,128)(2,1)}) %all-gather.7.cloned.1.call-update) | async-done | bytes 7372816 | tf_op jit(solution)/shard_map/all_gather | solution.py:67
  269.3 12.2 %copy.38 = bf16[3,3,8,1,51200]{4,2,1,0,3:T(8,128)(2,1)} copy(bf16[3,3,8,1,51200]{4,1,3,2,0:T(4,128)(2,1)} %all-gather.7.cloned.1.call-done) | data formatting | bytes 14745600 | tf_op jit(solution)/shard_map/all_gather | solution.py:67
  281.5 14.1 %reshape.50 = bf16[3,3,1280,320]{3,2,1,0:T(8,128)(2,1)} reshape(bf16[3,3,8,1,51200]{4,2,1,0,3:T(8,128)(2,1)} %copy.38) | data formatting | bytes 14745600 | tf_op jit(solution)/shard_map/reshape | solution.py:69
  295.6 4.0 fusion.38
  299.6 1.0 copy-done.1
  300.7 1.1 copy-done.3
  301.8 1.4 fusion.37
  303.3 2.8 add_bitcast_fusion.2
  306.1 0.6 slice.145
  306.7 2.8 fusion.44
  309.5 2.8 fusion.41
  312.2 1.5 fusion.43
  313.7 1.5 fusion.40
  315.1 2.8 add_bitcast_fusion.3
  317.9 4.4 convert_reduce_fusion
  322.4 0.3 copy.48
  322.6 0.8 reduce_sum.59
  323.7 20.5 %psum.30 = f32[8,16]{0,1:T(8,128)S(1)} all-reduce(f32[8,16]{0,1:T(8,128)S(1)} %reduce_sum.72), channel_id=1, replica_groups=mesh['wa'=4,'row'=8] {'row'}, use_global_device_ids=true, to_apply=%region_8.9 | all-reduce | flops 128 | bytes 1024 | tf_op jit(solution)/shard_map/psum | solution.py:34
  344.4 0.6 sub.33
  345.2 1.6 fusion.4
  346.8 0.3 copy.50
  347.0 0.8 reduce_sum.74
  348.1 19.3 %psum.31 = f32[8,16]{0,1:T(8,128)S(1)} all-reduce(f32[8,16]{0,1:T(8,128)S(1)} %reduce_sum.75), channel_id=1, replica_groups=mesh['wa'=4,'row'=8] {'row'}, use_global_device_ids=true, to_apply=%region_11.12 | all-reduce | flops 128 | bytes 1024 | tf_op jit(solution)/shard_map/psum | solution.py:36
  367.6 0.6 mul.57
  368.2 0.2 copy.51
  368.5 3.0 fusion.12
  371.4 42.5 %all-gather.11.cloned.1.call-done = bf16[3,3,8,1,51200]{4,1,3,2,0:T(4,128)(2,1)} async-done(((bf16[3,3,1,1,51200]{4,1,3,2,0:T(4,128)(2,1)}), bf16[3,3,8,1,51200]{4,1,3,2,0:T(4,128)(2,1)}) %all-gather.11.cloned.1.call-update) | async-done | bytes 7372816 | tf_op jit(solution)/shard_map/all_gather | solution.py:67
  413.9 12.1 %copy.52 = bf16[3,3,8,1,51200]{4,2,1,0,3:T(8,128)(2,1)} copy(bf16[3,3,8,1,51200]{4,1,3,2,0:T(4,128)(2,1)} %all-gather.11.cloned.1.call-done) | data formatting | bytes 14745600 | tf_op jit(solution)/shard_map/all_gather | solution.py:67
  426.0 14.0 %reshape.51 = bf16[3,3,1280,320]{3,2,1,0:T(8,128)(2,1)} reshape(bf16[3,3,8,1,51200]{4,2,1,0,3:T(8,128)(2,1)} %copy.52) | data formatting | bytes 14745600 | tf_op jit(solution)/shard_map/reshape | solution.py:69
  440.0 6.8 %all-gather.9.cloned.1.call-done = bf16[3,1280,512]{2,1,0:T(8,128)(2,1)} async-done(((bf16[3,320,512]{2,1,0:T(8,128)(2,1)}), bf16[3,1280,512]{2,1,0:T(8,128)(2,1)}) %all-gather.9.cloned.1.call-update) | async-done | bytes 3932176 | tf_op jit(solution)/shard_map/all_gather | solution.py:42
  446.8 2.0 fusion.51
  448.9 3.5 collective-permute-start.2
  452.4 1.8 collective-permute-start.3
  454.2 3.4 fusion.35
  457.6 1.5 fusion.32
  459.1 1.5 fusion.29
  460.6 48.2 %collective-permute-done.2 = bf16[1,1280,512]{2,1,0:T(8,128)(2,1)S(1)} collective-permute-done((bf16[1,1280,512]{2,1,0:T(8,128)(2,1)S(1)}, bf16[1,1280,512]{2,1,0:T(8,128)(2,1)S(1)}, u32[]{:S(2)}, u32[]{:S(2)}) %collective-permute-start.2) | collective-permute-done | bytes 1310752 | tf_op jit(solution)/shard_map/ppermute | solution.py:19
  508.8 1.4 fusion.30
  510.2 1.5 add_bitcast_fusion
  511.7 0.6 slice.157
  512.3 1.5 fusion.45
  513.7 1.5 fusion.33
  515.2 1.5 add_bitcast_fusion.1
  516.7 3.0 fusion.24
  (49 shorter events, 2.2 us)
Async XLA Ops:
  6.5 88.7 %all-gather.5.cloned.1.call-start = ((), (), s32[]{:S(2)}) async-start(), calls=%async_computation | async-start | bytes 4915200 | tf_op jit(solution)/shard_map/all_gather | solution.py:42
  9.0 26.8 %copy-start = (bf16[3,320,512]{2,1,0:T(8,128)(2,1)S(1)}, bf16[3,320,512]{2,1,0:T(8,128)(2,1)}, u32[]{:S(2)}) copy-start(bf16[3,320,512]{2,1,0:T(8,128)(2,1)} %param.9) | copy-start | bytes 2949124
  35.9 0.8 copy-start.2
  39.8 20.7 %copy-start.5 = (f32[320]{0:T(512)S(1)}, f32[320]{0:T(512)}, u32[]{:S(2)}) copy-start(f32[320]{0:T(512)} %param.11) | copy-start | bytes 3844
  39.8 20.7 %copy-start.6 = (f32[320]{0:T(512)S(1)}, f32[320]{0:T(512)}, u32[]{:S(2)}) copy-start(f32[320]{0:T(512)} %param.10) | copy-start | bytes 3844
  63.3 206.0 %all-gather.7.cloned.1.call-start = ((), (), s32[]{:S(2)}) async-start(), calls=%async_computation.1 | async-start | bytes 11059200 | tf_op jit(solution)/shard_map/all_gather | solution.py:67
  64.1 349.8 %all-gather.11.cloned.1.call-start = ((), (), s32[]{:S(2)}) async-start(), calls=%async_computation.3 | async-start | bytes 11059200 | tf_op jit(solution)/shard_map/all_gather | solution.py:67
  64.8 382.0 %all-gather.9.cloned.1.call-start = ((), (), s32[]{:S(2)}) async-start(), calls=%async_computation.2 | async-start | bytes 4915200 | tf_op jit(solution)/shard_map/all_gather | solution.py:42
  97.1 198.5 %collective-permute-start = (bf16[1,1280,512]{2,1,0:T(8,128)(2,1)S(1)}, bf16[1,1280,512]{2,1,0:T(8,128)(2,1)}, u32[]{:S(2)}, u32[]{:S(2)}) collective-permute-start(bf16[1,1280,512]{2,1,0:T(8,128)(2,1)S(1)} %get-tuple-element.8), channel_id=1, source_target_pairs={{0,1},{1,2},{2,3},{3,4},{4,5},{5,6},{6,7},{8,9},{9,10},{10,11},{11... | collective-permute-start | bytes 3932168 | tf_op jit(solution)/shard_map/ppermute | solution.py:19
  101.5 201.7 %collective-permute-start.1 = (bf16[1,1280,512]{2,1,0:T(8,128)(2,1)S(1)}, bf16[1,1280,512]{2,1,0:T(8,128)(2,1)}, u32[]{:S(2)}, u32[]{:S(2)}) collective-permute-start(bf16[1,1280,512]{2,1,0:T(8,128)(2,1)S(1)} %get-tuple-element.7), channel_id=1, source_target_pairs={{1,0},{2,1},{3,2},{4,3},{5,4},{6,5},{7,6},{9,8},{10,9},{11,10},{12... | collective-permute-start | bytes 3932168 | tf_op jit(solution)/shard_map/ppermute | solution.py:21
  295.6 5.0 copy-start.1
  295.6 6.2 %copy-start.3 = (bf16[3,1280,512]{2,1,0:T(8,128)(2,1)S(1)}, bf16[3,1280,512]{2,1,0:T(8,128)(2,1)}, u32[]{:S(2)}) copy-start(bf16[3,1280,512]{2,1,0:T(8,128)(2,1)} %all-gather.5.cloned.1.call-done) | copy-start | bytes 11796484
  315.1 2.8 copy-start.9
  347.8 20.6 %copy-start.7 = (f32[320]{0:T(512)S(1)}, f32[320]{0:T(512)}, u32[]{:S(2)}) copy-start(f32[320]{0:T(512)} %param.15) | copy-start | bytes 3844
  347.9 20.6 %copy-start.8 = (f32[320]{0:T(512)S(1)}, f32[320]{0:T(512)}, u32[]{:S(2)}) copy-start(f32[320]{0:T(512)} %param.14) | copy-start | bytes 3844
  446.8 7.4 %copy-start.4 = (bf16[3,1280,512]{2,1,0:T(8,128)(2,1)S(1)}, bf16[3,1280,512]{2,1,0:T(8,128)(2,1)}, u32[]{:S(2)}) copy-start(bf16[3,1280,512]{2,1,0:T(8,128)(2,1)} %all-gather.9.cloned.1.call-done) | copy-start | bytes 11796484
  448.9 59.9 %collective-permute-start.2 = (bf16[1,1280,512]{2,1,0:T(8,128)(2,1)S(1)}, bf16[1,1280,512]{2,1,0:T(8,128)(2,1)S(1)}, u32[]{:S(2)}, u32[]{:S(2)}) collective-permute-start(bf16[1,1280,512]{2,1,0:T(8,128)(2,1)S(1)} %get-tuple-element.6), channel_id=1, source_target_pairs={{0,1},{1,2},{2,3},{3,4},{4,5},{5,6},{6,7},{8,9},{9,10},{10,11},{11... | collective-permute-start | bytes 3932168 | tf_op jit(solution)/shard_map/ppermute | solution.py:19
  452.4 5.3 slice-start
  452.4 5.3 slice-start.1
  452.4 5.3 slice-start.2
  452.4 57.8 %collective-permute-start.3 = (bf16[1,1280,512]{2,1,0:T(8,128)(2,1)S(1)}, bf16[1,1280,512]{2,1,0:T(8,128)(2,1)S(1)}, u32[]{:S(2)}, u32[]{:S(2)}) collective-permute-start(bf16[1,1280,512]{2,1,0:T(8,128)(2,1)S(1)} %get-tuple-element.5), channel_id=1, source_target_pairs={{1,0},{2,1},{3,2},{4,3},{5,4},{6,5},{7,6},{9,8},{10,9},{11,10},{12... | collective-permute-start | bytes 3932168 | tf_op jit(solution)/shard_map/ppermute | solution.py:21
  515.2 1.5 copy-start.10
Sparse Core Ops, SparseCore 0:
  63.5 31.6 all-gather.4
  97.4 171.8 all-gather.6
  271.5 142.3 all-gather.10
  415.3 31.4 all-gather.8
where the time goes:
time: 536 us; the launch traced here: 527 us
  waiting for transfers between devices  296 us (55%)
  blocking collectives  80.6 us (15%)
  local copies, waits for them, and re-layouts  74.6 us (14%)
  matrix products  40.5 us (8%)
  between operations  14.1 us (3%)
  starting transfers between devices  11.1 us (2%)
  other arithmetic  9.98 us (2%)
    all_gather x2, waiting for transfers between devices, convolve(): weights_piece = lax.all_gather(kernel, 'row', axis=2, tiled=True)  209 us
    ppermute x2, waiting for transfers between devices, padded_2(): lax.ppermute(tail, axis, [(i, (i + 1) % count) for i in range(ends)])  48.2 us
    psum x2, blocking collectives, activate(): center = lax.psum(jnp.sum(grouped, axis=(0, 2, 4)), 'row') / total_count  43.9 us
    dot_general x18, matrix products, convolve(): jnp.einsum('rcw,co->row', window, weight_slab[row_tap, col_tap], preferre...  40.5 us
    all_gather x2, waiting for transfers between devices, panel_of(): wide_rows = lax.all_gather(shard, 'wa', axis=1, tiled=True)  37.2 us
    psum x2, blocking collectives, activate(): lax.psum(jnp.sum(jnp.square(offset), axis=(0, 2, 4)), 'row') / total_count  36.6 us
    reshape x2, local copies, waits for them, and re-layouts, convolve(): weight_slab = weights_piece.reshape(3, 3, inner_count, out_chans)  28.1 us
    all_gather x2, local copies, waits for them, and re-layouts, convolve(): weights_piece = lax.all_gather(kernel, 'row', axis=2, tiled=True)  24.3 us
  transfers between devices with their start and end apart: 8, of which 5 were waited for; matrix products, arithmetic and copies ran while one was open for 18% of the time, Pallas kernels for 0%

commit v1 on v0

v1 whole, which is shorter than its diff:
```python
import jax
import jax.numpy as jnp
from jax import lax
from jax.experimental import pallas as pl
from jax.experimental.pallas import tpu as pltpu
from jax.sharding import PartitionSpec as P


C = 1280
GROUPS = 32
WIDTH = 32
GROUP_SIZE = C // GROUPS
TAPS = 3
EPS = 1e-05
VMEM_LIMIT = 60 * 1024 * 1024


def params(**extra):
    return pltpu.CompilerParams(vmem_limit_bytes=VMEM_LIMIT, **extra)


def xor_pairs(count, bit):
    return [(i, i ^ bit) for i in range(count)]


def image_select(lanes, images=128):
    lane = lax.broadcasted_iota(jnp.int32, (lanes, images), 0) // WIDTH
    return (lane == lax.broadcasted_iota(jnp.int32, (lanes, images), 1)).astype(jnp.float32)


def image_sum(value, select):
    return jnp.dot(value, select, precision=lax.Precision.HIGHEST, preferred_element_type=jnp.float32)


def image_spread(value, select):
    return lax.dot_general(
        value, select, (((1,), (1,)), ((), ())), precision=lax.Precision.HIGHEST, preferred_element_type=jnp.float32
    )


def stats_body(x_ref, out_ref, total_ref):
    rows, chans, lanes = x_ref.shape
    groups = chans // GROUP_SIZE
    count = rows * GROUP_SIZE * WIDTH
    select = image_select(lanes)
    spans = [slice(g * GROUP_SIZE, (g + 1) * GROUP_SIZE) for g in range(groups)]
    for g in range(groups):
        part = x_ref[:, spans[g], :].astype(jnp.float32)
        total_ref[g : g + 1, :] = jnp.sum(jnp.sum(part, axis=0), axis=0, keepdims=True)
    mean = image_sum(total_ref[...], select) / count
    out_ref[0] = mean
    wide = image_spread(mean, select)
    for g in range(groups):
        off = x_ref[:, spans[g], :].astype(jnp.float32) - wide[None, g : g + 1, :]
        total_ref[g : g + 1, :] = jnp.sum(jnp.sum(off * off, axis=0), axis=0, keepdims=True)
    out_ref[1] = image_sum(total_ref[...], select)


def local_stats(x):
    groups = x.shape[1] // GROUP_SIZE
    return pl.pallas_call(
        stats_body,
        out_shape=jax.ShapeDtypeStruct((2, groups, 128), jnp.float32),
        scratch_shapes=[pltpu.VMEM((groups, x.shape[2]), jnp.float32)],
        compiler_params=params(),
        name="stats",
    )(x)


def exchanged(stats):
    n_row = lax.axis_size("row")
    return [stats] + [lax.ppermute(stats, "row", xor_pairs(n_row, k)) for k in range(1, n_row)]


def norm_body(count, n_row, flag_ref, x_ref, above_ref, below_ref, gain_ref, shift_ref, *refs):
    stats_refs = refs[:n_row]
    out_refs = refs[n_row:]
    rows, chans, lanes = x_ref.shape
    groups = chans // GROUP_SIZE
    width = out_refs[0].shape[1]
    select = image_select(lanes)
    center = sum(ref[0] for ref in stats_refs) / n_row
    square = sum(ref[1] for ref in stats_refs) + count * sum(jnp.square(ref[0] - center) for ref in stats_refs)
    scale = lax.rsqrt(square / (count * n_row) + EPS)
    wide_center = image_spread(center, select)
    wide_scale = image_spread(scale, select)
    for g in range(groups):
        span = slice(g * GROUP_SIZE, (g + 1) * GROUP_SIZE)
        out_ref = out_refs[g * GROUP_SIZE // width]
        start = g * GROUP_SIZE % width
        mean = wide_center[g : g + 1, :]
        inv = wide_scale[g : g + 1, :]
        gain = gain_ref[span, :]
        shift = shift_ref[span, :]

        def act(value):
            v = (value.astype(jnp.float32) - mean) * inv * gain + shift
            return v / (1.0 + jnp.exp(-v))

        here = slice(start, start + GROUP_SIZE)
        out_ref[0, here, :] = (act(above_ref[0, span, :]) * flag_ref[0]).astype(jnp.bfloat16)
        for r in range(rows):
            out_ref[r + 1, here, :] = act(x_ref[r, span, :]).astype(jnp.bfloat16)
        out_ref[rows + 1, here, :] = (act(below_ref[0, span, :]) * flag_ref[1]).astype(jnp.bfloat16)


def edges_of(x):
    n_row = lax.axis_size("row")
    above = lax.ppermute(x[-1:], "row", [(i, i + 1) for i in range(n_row - 1)])
    below = lax.ppermute(x[:1], "row", [(i + 1, i) for i in range(n_row - 1)])
    return above, below


def surroundings(x):
    return edges_of(x), exchanged(local_stats(x))


def activate(x, around, gain, shift):
    n_row = lax.axis_size("row")
    rows, chans, lanes = x.shape
    ci = C // n_row
    count = rows * GROUP_SIZE * WIDTH
    (above, below), stats = around
    r = lax.axis_index("row")
    flags = jnp.stack([r > 0, r < n_row - 1]).astype(jnp.float32)
    vmem = pl.BlockSpec(memory_space=pltpu.VMEM)
    return pl.pallas_call(
        lambda *refs: norm_body(count, n_row, *refs),
        in_specs=[pl.BlockSpec(memory_space=pltpu.SMEM)] + [vmem] * (5 + n_row),
        out_shape=[jax.ShapeDtypeStruct((rows + 2, ci, lanes), jnp.bfloat16)] * (chans // ci),
        compiler_params=params(),
        name="norm",
    )(flags, x, above, below, gain[:, None], shift[:, None], *stats)


def gather_wa(parts):
    n_wa = lax.axis_size("wa")
    pieces = {0: list(parts)}
    bit = n_wa // 2
    while bit:
        for k in sorted(pieces):
            pieces[k | bit] = [lax.ppermute(p, "wa", xor_pairs(n_wa, bit)) for p in pieces[k]]
        bit //= 2
    return [pieces[k] for k in range(n_wa)]


def prepared(kernel, ci, co):
    flat = kernel.reshape(TAPS, TAPS * ci, co)
    turned = jnp.transpose(flat, (2, 0, 1))
    depth = -(-TAPS * ci // 128) * 128
    turned = jnp.pad(turned, ((0, 0), (0, 0), (0, depth - TAPS * ci)))
    return turned.reshape(co, TAPS * depth)


def ring_order(n):
    return list(range(0, n, 2)) + list(range(n - 1, 0, -2))


def ring_blocks():
    n = lax.axis_size("row")
    r = lax.axis_index("row")
    place = jnp.where(r % 2 == 0, r // 2, n - 1 - r // 2)
    shifts = [0]
    for s in range(1, n // 2):
        shifts += [n - s, s]
    shifts.append(n // 2)
    at = (place + jnp.array(shifts, jnp.int32)) % n
    return jnp.where(2 * at < n, 2 * at, 2 * (n - at) - 1)


def ring(own, hold):
    n = lax.axis_size("row")
    order = ring_order(n)
    up = [(order[i], order[(i + 1) % n]) for i in range(n)]
    down = [(d, s) for s, d in up]
    chunks = [own]
    a = b = own
    for s in range(1, n // 2 + 1):
        if s in hold:
            a, b, _ = lax.optimization_barrier((a, b, hold[s]))
        if s == n // 2:
            half = own.shape[0] // 2
            a, b = a[:half], b[half:]
        a = lax.ppermute(a, "row", up)
        b = lax.ppermute(b, "row", down)
        chunks += [a, b]
    return chunks


def conv_body(early, n_chunks, n_wa, idx_ref, chunk_refs, act_refs, acc_ref, wbuf, abuf, xbuf, wsem, asem):
    rows, co, lanes = acc_ref.shape
    ci = abuf.shape[2]
    depth = xbuf.shape[1]
    per_shard = n_chunks // n_wa
    me = idx_ref[n_chunks]

    def piece_of(c):
        return (idx_ref[c] // per_shard) ^ me

    def mine(c):
        soon = jnp.logical_and(piece_of(c) < 2, c < n_chunks - 1)
        return soon if early else jnp.logical_not(soon)

    for c in range(n_chunks - 1 if early else n_chunks):

        @pl.when(mine(c))
        def _():
            if c < n_chunks - 1:
                pltpu.make_async_copy(chunk_refs[c], wbuf.at[c], wsem.at[c]).start()
            else:
                half = co // 2
                for i in range(2):
                    pltpu.make_async_copy(
                        chunk_refs[c + i], wbuf.at[c, pl.ds(i * half, half), :], wsem.at[c]
                    ).start()
            slot = piece_of(c) * per_shard + idx_ref[c] % per_shard
            for k in range(len(act_refs)):

                @pl.when(slot == k)
                def _():
                    pltpu.make_async_copy(act_refs[k], abuf.at[c], asem.at[c]).start()

    if depth > TAPS * ci:
        xbuf[:, TAPS * ci :, :] = jnp.zeros((rows + 2, depth - TAPS * ci, lanes), jnp.bfloat16)
    column = lax.broadcasted_iota(jnp.int32, (ci, lanes), 1) % WIDTH

    def step(c, carry):
        @pl.when(mine(c))
        def _():
            pltpu.make_async_copy(act_refs[0], abuf.at[c], asem.at[c]).wait()
            for r in range(rows + 2):
                v = abuf[c, r]
                zero = jnp.zeros_like(v)
                xbuf[r, 0:ci, :] = jnp.where(column == 0, zero, pltpu.roll(v, 1, 1))
                xbuf[r, ci : 2 * ci, :] = v
                xbuf[r, 2 * ci : 3 * ci, :] = jnp.where(column == WIDTH - 1, zero, pltpu.roll(v, lanes - 1, 1))
            pltpu.make_async_copy(chunk_refs[0], wbuf.at[c], wsem.at[c]).wait()
            for r in range(rows):
                panel = xbuf[r : r + TAPS].reshape(TAPS * depth, lanes)
                acc_ref[r] += jnp.dot(wbuf[c], panel, preferred_element_type=jnp.float32)

        return carry

    lax.fori_loop(0, n_chunks - 1 if early else n_chunks, step, 0)


def conv_part(early, idx, chunks, acts, acc, bias):
    n_wa = lax.axis_size("wa")
    n_chunks = lax.axis_size("row")
    rows, ci, lanes = acts[0].shape
    rows -= 2
    co, kdim = chunks[0].shape
    depth = kdim // TAPS
    n_in = len(chunks) + len(acts)

    def body(idx_ref, *refs):
        refs = list(refs)
        chunk_refs = refs[: len(chunks)]
        act_refs = refs[len(chunks) : n_in]
        rest = refs[n_in:]
        if early:
            acc_ref, *scratch = rest
            acc_ref[...] = jnp.zeros(acc_ref.shape, jnp.float32)
        else:
            acc_in, bias_ref, out_ref, acc_ref, *scratch = rest
            acc_ref[...] = acc_in[...] + bias_ref[...][None]
        conv_body(early, n_chunks, n_wa, idx_ref, chunk_refs, act_refs, acc_ref, *scratch)
        if not early:
            out_ref[...] = acc_ref[...].astype(jnp.bfloat16)

    any_spec = pl.BlockSpec(memory_space=pl.ANY)
    full = pl.BlockSpec(memory_space=pltpu.VMEM)
    in_specs = [pl.BlockSpec(memory_space=pltpu.SMEM)] + [any_spec] * n_in
    args = [idx] + chunks + acts
    scratch = []
    if not early:
        in_specs += [full, full]
        args += [acc, bias[:, None]]
        scratch.append(pltpu.VMEM((rows, co, lanes), jnp.float32))
    scratch += [
        pltpu.VMEM((n_chunks, co, kdim), jnp.bfloat16),
        pltpu.VMEM((n_chunks, rows + 2, ci, lanes), jnp.bfloat16),
        pltpu.VMEM((rows + 2, depth, lanes), jnp.bfloat16),
        pltpu.SemaphoreType.DMA((n_chunks,)),
        pltpu.SemaphoreType.DMA((n_chunks,)),
    ]
    return pl.pallas_call(
        body,
        in_specs=in_specs,
        out_specs=full,
        out_shape=jax.ShapeDtypeStruct((rows, co, lanes), jnp.float32 if early else jnp.bfloat16),
        scratch_shapes=scratch,
        compiler_params=params(),
        name="conv",
    )(*args)


def convolve(parts, chunks, idx, bias):
    pieces = gather_wa(parts)
    near = pieces[0] + pieces[1]
    every = [p for piece in pieces for p in piece]
    acc = conv_part(True, idx, chunks[:-2], near, None, None)
    return conv_part(False, idx, chunks, every, acc, bias)


def per_device(
    activations,
    gain_one,
    shift_one,
    kernel_one,
    bias_one,
    gain_two,
    shift_two,
    kernel_two,
    bias_two,
):
    co = activations.shape[1]
    ci = kernel_one.shape[4] // co
    idx = jnp.concatenate([ring_blocks(), lax.axis_index("wa").astype(jnp.int32)[None]])
    own_one = prepared(kernel_one, ci, co)
    own_two = prepared(kernel_two, ci, co)
    around = surroundings(activations)
    chunks_one = ring(own_one, {2: (around, own_two)})
    first = activate(activations, around, gain_one, shift_one)
    hidden = convolve(first, chunks_one, idx, bias_one)
    around = surroundings(hidden)
    chunks_two = ring(own_two, {2: around})
    second = activate(hidden, around, gain_two, shift_two)
    return convolve(second, chunks_two, idx, bias_two)


def solution(mesh):
    placed = (
        P("row", "wa", None),
        P("wa"),
        P("wa"),
        P(None, None, "row", "wa", None),
        P("wa"),
        P("wa"),
        P("wa"),
        P(None, None, "row", "wa", None),
        P("wa"),
    )

    return jax.shard_map(
        per_device, mesh=mesh, in_specs=placed, out_specs=P("row", "wa", None), check_vma=False
    )
```

time: 536 us -> 271 us (0.51); the launches traced: 527 us -> 270 us
  waiting for transfers between devices: 296 us -> 111 us
  blocking collectives: 80.6 us -> 0 us
  Pallas kernels: 0 us -> 66.3 us
  starting transfers between devices: 11.1 us -> 69.1 us
  local copies, waits for them, and re-layouts: 74.6 us -> 21.7 us
  matrix products: 40.5 us -> 0 us
  between operations: 14.1 us -> 0.66 us
  other arithmetic: 9.98 us -> 1.23 us
    all_gather x4 -> x0, waiting for transfers between devices: 246 us -> none  [the longest x2 209 us: convolve(): weights_piece = lax.all_gather(kernel, 'row', axis=2, tiled=True)]
    psum x4 -> x0, blocking collectives: 80.6 us -> none  [the longest x2 43.9 us: activate(): center = lax.psum(jnp.sum(grouped, axis=(0, 2, 4)), 'row') / total_count]
    pallas_call x0 -> x8, Pallas kernels: none -> 66.3 us  [the longest x4 51.4 us: conv_part(): pl.pallas_call(body, in_specs=in_specs, out_specs=full, out_shape=jax.Sha...]
    ppermute x4 -> x46, waiting for transfers between devices: 48.2 us -> 111 us  [the longest x12 46.5 us: gather_wa(): lax.ppermute(p, 'wa', xor_pairs(n_wa, bit))]
    ppermute x4 -> x46, starting transfers between devices: 11 us -> 69.1 us  [the longest x14 37.3 us: exchanged(): lax.ppermute(stats, 'row', xor_pairs(n_row, k))]
    dot_general x18 -> x0, matrix products: 40.5 us -> none  [convolve(): jnp.einsum('rcw,co->row', window, weight_slab[row_tap, col_tap], preferre...]
    all_gather x2 -> x0, local copies, waits for them, and re-layouts: 24.3 us -> none  [convolve(): weights_piece = lax.all_gather(kernel, 'row', axis=2, tiled=True)]
    reshape x2 -> x4, local copies, waits for them, and re-layouts: 28.1 us -> 7.86 us  [the longest x2 5.72 us: prepared(): flat = kernel.reshape(TAPS, TAPS * ci, co)]
  transfers between devices with their start and end apart: 8 -> 46, of which waited for: 5 -> 16; matrix products, arithmetic and copies ran while one was open for 18% -> 6% of each run, Pallas kernels for 0% -> 20%
where the time goes in v1:
time: 271 us; the launch traced here: 270 us
  waiting for transfers between devices  111 us (41%)
  starting transfers between devices  69.1 us (25%)
  Pallas kernels  66.3 us (24%)
  local copies, waits for them, and re-layouts  21.7 us (8%)
    pallas_call x4, Pallas kernels, conv_part(): pl.pallas_call(body, in_specs=in_specs, out_specs=full, out_shape=jax.Sha...  51.4 us
    ppermute x12, waiting for transfers between devices, gather_wa(): lax.ppermute(p, 'wa', xor_pairs(n_wa, bit))  46.5 us
    ppermute x14, starting transfers between devices, exchanged(): lax.ppermute(stats, 'row', xor_pairs(n_row, k))  37.3 us
    ppermute x14, waiting for transfers between devices, exchanged(): lax.ppermute(stats, 'row', xor_pairs(n_row, k))  33.3 us
    ppermute x8, waiting for transfers between devices, ring(): a = lax.ppermute(a, 'row', up)  31.1 us
    ppermute x8, starting transfers between devices, ring(): a = lax.ppermute(a, 'row', up)  11.7 us
    pallas_call x2, Pallas kernels, activate(): pl.pallas_call(lambda *refs: norm_body(count, n_row, *refs), in_specs=[pl...  8.78 us
    ppermute x2, starting transfers between devices, edges_of(): above = lax.ppermute(x[-1:], 'row', [(i, i + 1) for i in range(n_row - 1)])  6.34 us
  transfers between devices with their start and end apart: 46, of which 16 were waited for; matrix products, arithmetic and copies ran while one was open for 6% of the time, Pallas kernels for 20%

profile of v1, /device:TPU:0, one launch (start us, length us, event | category | flops | bytes accessed | tf_op | source)
XLA Modules:
  0.0 270.0 jit_solution(16078068111972235810)
XLA Ops:
  0.0 2.9 %reshape.14 = bf16[3,480,320]{2,1,0:T(8,128)(2,1)S(1)} reshape(bf16[3,3,1,1,51200]{4,1,3,2,0:T(4,128)(2,1)} %param.13) | data formatting | bytes 1843200 | tf_op jit(solution)/shard_map/reshape | solution.py:148
  3.6 3.1 %collective-permute-start.2 = (bf16[320,1536]{1,0:T(8,128)(2,1)S(1)}, bf16[320,1536]{1,0:T(8,128)(2,1)S(1)}, u32[]{:S(2)}, u32[]{:S(2)}) collective-permute-start(bf16[320,1536]{1,0:T(8,128)(2,1)S(1)} %copy.20.refs_0_), channel_id=1, source_target_pairs={{0,2},{2,4},{4,6},{6,7},{7,5},{5,3},{3,1},{1,0},{8,10},{10,12},{12... | collective-permute-start | bytes 2949128 | tf_op jit(solution)/shard_map/ppermute | solution.py:184
  6.8 0.9 fusion.2
  7.7 3.8 %collective-permute-start.4 = (bf16[1,320,512]{2,1,0:T(8,128)(2,1)}, bf16[1,320,512]{2,1,0:T(8,128)(2,1)S(1)}, u32[]{:S(2)}, u32[]{:S(2)}) collective-permute-start(bf16[1,320,512]{2,1,0:T(8,128)(2,1)} %get-tuple-element.24), channel_id=1, source_target_pairs={{0,1},{1,2},{2,3},{3,4},{4,5},{5,6},{6,7},{8,9},{9,10},{10,11},{11... | collective-permute-start | bytes 983048 | tf_op jit(solution)/shard_map/ppermute | solution.py:109
  11.5 1.3 collective-permute-start.5
  12.8 3.1 %stats.2.refs_6_ = f32[2,8,128]{2,1,0:T(8,128)} custom-call(bf16[3,320,512]{2,1,0:T(8,128)(2,1)} %refs_1_.1), custom_call_target="tpu_custom_call" | custom-call | tf_op jit(solution)/shard_map/stats/pallas_call | solution.py:61
  15.9 4.7 %collective-permute-start.10 = (f32[2,8,128]{2,1,0:T(8,128)}, f32[2,8,128]{2,1,0:T(8,128)S(1)}, u32[]{:S(2)}, u32[]{:S(2)}) collective-permute-start(f32[2,8,128]{2,1,0:T(8,128)} %stats.2.refs_6_), channel_id=1, source_target_pairs={{0,5},{1,4},{2,7},{3,6},{4,1},{5,0},{6,3},{7,2},{8,13},{9,12},{10,... | collective-permute-start | bytes 24584 | tf_op jit(solution)/shard_map/ppermute | solution.py:72
  20.5 10.4 %collective-permute-done.10.refs_11_ = f32[2,8,128]{2,1,0:T(8,128)S(1)} collective-permute-done((f32[2,8,128]{2,1,0:T(8,128)}, f32[2,8,128]{2,1,0:T(8,128)S(1)}, u32[]{:S(2)}, u32[]{:S(2)}) %collective-permute-start.10) | collective-permute-done | bytes 8224 | tf_op jit(solution)/shard_map/ppermute | solution.py:72
  31.0 9.7 %collective-permute-start.11 = (f32[2,8,128]{2,1,0:T(8,128)}, f32[2,8,128]{2,1,0:T(8,128)S(1)}, u32[]{:S(2)}, u32[]{:S(2)}) collective-permute-start(f32[2,8,128]{2,1,0:T(8,128)} %stats.2.refs_6_), channel_id=1, source_target_pairs={{0,6},{1,7},{2,4},{3,5},{4,2},{5,3},{6,0},{7,1},{8,14},{9,15},{10,... | collective-permute-start | bytes 24584 | tf_op jit(solution)/shard_map/ppermute | solution.py:72
  40.7 1.8 collective-permute-done.11.refs_12_
  42.5 2.4 collective-permute-start.12
  44.9 4.1 %collective-permute-done.12.refs_13_ = f32[2,8,128]{2,1,0:T(8,128)S(1)} collective-permute-done((f32[2,8,128]{2,1,0:T(8,128)}, f32[2,8,128]{2,1,0:T(8,128)S(1)}, u32[]{:S(2)}, u32[]{:S(2)}) %collective-permute-start.12) | collective-permute-done | bytes 8224 | tf_op jit(solution)/shard_map/ppermute | solution.py:72
  49.1 3.0 %collective-permute-start.6 = (f32[2,8,128]{2,1,0:T(8,128)}, f32[2,8,128]{2,1,0:T(8,128)S(1)}, u32[]{:S(2)}, u32[]{:S(2)}) collective-permute-start(f32[2,8,128]{2,1,0:T(8,128)} %stats.2.refs_6_), channel_id=1, source_target_pairs={{0,1},{1,0},{2,3},{3,2},{4,5},{5,4},{6,7},{7,6},{8,9},{9,8},{10,11... | collective-permute-start | bytes 24584 | tf_op jit(solution)/shard_map/ppermute | solution.py:72
  52.0 1.8 collective-permute-done.6.refs_7_
  53.9 3.9 %collective-permute-done.7.refs_8_ = f32[2,8,128]{2,1,0:T(8,128)S(1)} collective-permute-done((f32[2,8,128]{2,1,0:T(8,128)}, f32[2,8,128]{2,1,0:T(8,128)S(1)}, u32[]{:S(2)}, u32[]{:S(2)}) %collective-permute-start.7) | collective-permute-done | bytes 8224 | tf_op jit(solution)/shard_map/ppermute | solution.py:72
  57.8 1.5 collective-permute-start.8
  59.2 3.3 %collective-permute-done.8.refs_9_ = f32[2,8,128]{2,1,0:T(8,128)S(1)} collective-permute-done((f32[2,8,128]{2,1,0:T(8,128)}, f32[2,8,128]{2,1,0:T(8,128)S(1)}, u32[]{:S(2)}, u32[]{:S(2)}) %collective-permute-start.8) | collective-permute-done | bytes 8224 | tf_op jit(solution)/shard_map/ppermute | solution.py:72
  62.5 1.4 collective-permute-start.9
  63.9 2.9 %reshape.12 = bf16[3,480,320]{2,1,0:T(8,128)(2,1)S(1)} reshape(bf16[3,3,1,1,51200]{4,1,3,2,0:T(4,128)(2,1)} %param.17) | data formatting | bytes 1843200 | tf_op jit(solution)/shard_map/reshape | solution.py:148
  66.8 1.1 pad.7
  68.1 2.1 collective-permute-start.13
  70.9 0.8 broadcast_in_dim.29.refs_5_
  72.4 4.4 %norm.2 = (bf16[5,160,512]{2,1,0:T(8,128)(2,1)}, bf16[5,160,512]{2,1,0:T(8,128)(2,1)}) custom-call(f32[2]{0:T(128)} %add_convert_fusion.refs_0_, bf16[3,320,512]{2,1,0:T(8,128)(2,1)} %refs_1_.1, bf16[1,320,512]{2,1,0:T(8,128)(2,1)} %copy-done.14, bf16[1,320,512]{2,1,0:T(8,128)(2,1)} %collective-permute-done.5.refs_3_, f32[320,1]{1,0:T(8,128)} %broadcast_in_dim.28.refs_4_, ...), custom_call_target="tpu_custom_call" | custom-call | tf_op jit(solution)/shard_map/norm/pallas_call | solution.py:127
  76.8 1.5 collective-permute-start.21
  78.8 11.1 %collective-permute-done.13.refs_3_ = bf16[320,1536]{1,0:T(8,128)(2,1)S(1)} collective-permute-done((bf16[320,1536]{1,0:T(8,128)(2,1)S(1)}, bf16[320,1536]{1,0:T(8,128)(2,1)S(1)}, u32[]{:S(2)}, u32[]{:S(2)}) %collective-permute-start.13) | collective-permute-done | bytes 983072 | tf_op jit(solution)/shard_map/ppermute | solution.py:184
  90.0 2.0 collective-permute-start.15
  92.1 6.2 %collective-permute-done.21.refs_13_ = bf16[5,160,512]{2,1,0:T(8,128)(2,1)} collective-permute-done((bf16[5,160,512]{2,1,0:T(8,128)(2,1)}, bf16[5,160,512]{2,1,0:T(8,128)(2,1)}, u32[]{:S(2)}, u32[]{:S(2)}) %collective-permute-start.21) | collective-permute-done | bytes 819232 | tf_op jit(solution)/shard_map/ppermute | solution.py:142
  98.2 9.0 %collective-permute-done.22.refs_14_ = bf16[5,160,512]{2,1,0:T(8,128)(2,1)} collective-permute-done((bf16[5,160,512]{2,1,0:T(8,128)(2,1)}, bf16[5,160,512]{2,1,0:T(8,128)(2,1)}, u32[]{:S(2)}, u32[]{:S(2)}) %collective-permute-start.22) | collective-permute-done | bytes 819232 | tf_op jit(solution)/shard_map/ppermute | solution.py:142
  107.7 0.8 slice.32
  108.5 1.7 collective-permute-start.17
  110.3 0.8 slice.33
  111.1 0.9 copy-done.11
  112.3 1.5 copy.25.refs_0_
  113.9 1.8 collective-permute-start
  117.3 12.6 %conv.4.refs_17_ = f32[3,320,512]{2,1,0:T(8,128)} custom-call(s32[9]{0:T(128)} %pad_add_fusion.idx_ref, bf16[320,1536]{1,0:T(8,128)(2,1)} %copy-done.1, bf16[320,1536]{1,0:T(8,128)(2,1)} %copy-done.9, bf16[320,1536]{1,0:T(8,128)(2,1)} %collective-permute-done.3.refs_2_, bf16[320,1536]{1,0:T(8,128)(2,1)} %copy-done.10, ...), custom_call_target="tpu_custom_call" | custom-call | tf_op jit(solution)/shard_map/conv/pallas_call | solution.py:287
  130.0 13.1 %conv.5.x_ref.refs_1_ = bf16[3,320,512]{2,1,0:T(8,128)(2,1)} custom-call(s32[9]{0:T(128)} %pad_add_fusion.idx_ref, bf16[320,1536]{1,0:T(8,128)(2,1)} %copy-done.1, bf16[320,1536]{1,0:T(8,128)(2,1)} %copy-done.9, bf16[320,1536]{1,0:T(8,128)(2,1)} %collective-permute-done.3.refs_2_, bf16[320,1536]{1,0:T(8,128)(2,1)} %copy-done.10, ...), custom_call_target="tpu_custom_call" | custom-call | tf_op jit(solution)/shard_map/conv/pallas_call | solution.py:287
  143.1 2.0 fusion.1
  145.1 2.5 collective-permute-start.25
  147.6 1.5 collective-permute-start.26
  149.0 3.1 %stats.3.refs_6_ = f32[2,8,128]{2,1,0:T(8,128)} custom-call(bf16[3,320,512]{2,1,0:T(8,128)(2,1)} %conv.5.x_ref.refs_1_), custom_call_target="tpu_custom_call" | custom-call | tf_op jit(solution)/shard_map/stats/pallas_call | solution.py:61
  152.1 3.0 %collective-permute-start.27 = (f32[2,8,128]{2,1,0:T(8,128)}, f32[2,8,128]{2,1,0:T(8,128)S(1)}, u32[]{:S(2)}, u32[]{:S(2)}) collective-permute-start(f32[2,8,128]{2,1,0:T(8,128)} %stats.3.refs_6_), channel_id=1, source_target_pairs={{0,1},{1,0},{2,3},{3,2},{4,5},{5,4},{6,7},{7,6},{8,9},{9,8},{10,11... | collective-permute-start | bytes 24584 | tf_op jit(solution)/shard_map/ppermute | solution.py:72
  155.1 1.5 collective-permute-start.28
  156.7 1.5 collective-permute-start.29
  158.1 3.2 %collective-permute-done.27.refs_7_ = f32[2,8,128]{2,1,0:T(8,128)S(1)} collective-permute-done((f32[2,8,128]{2,1,0:T(8,128)}, f32[2,8,128]{2,1,0:T(8,128)S(1)}, u32[]{:S(2)}, u32[]{:S(2)}) %collective-permute-start.27) | collective-permute-done | bytes 8224 | tf_op jit(solution)/shard_map/ppermute | solution.py:72
  161.3 3.9 %collective-permute-start.30 = (f32[2,8,128]{2,1,0:T(8,128)}, f32[2,8,128]{2,1,0:T(8,128)S(1)}, u32[]{:S(2)}, u32[]{:S(2)}) collective-permute-start(f32[2,8,128]{2,1,0:T(8,128)} %stats.3.refs_6_), channel_id=1, source_target_pairs={{0,4},{1,5},{2,6},{3,7},{4,0},{5,1},{6,2},{7,3},{8,12},{9,13},{10,... | collective-permute-start | bytes 24584 | tf_op jit(solution)/shard_map/ppermute | solution.py:72
  165.2 0.9 collective-permute-start.31
  166.1 1.9 collective-permute-start.32
  168.1 2.0 collective-permute-start.33
  170.0 0.8 collective-permute-done.31.refs_11_
  170.9 0.9 collective-permute-done.32.refs_12_
  171.8 2.9 %collective-permute-done.33.refs_13_ = f32[2,8,128]{2,1,0:T(8,128)S(1)} collective-permute-done((f32[2,8,128]{2,1,0:T(8,128)}, f32[2,8,128]{2,1,0:T(8,128)S(1)}, u32[]{:S(2)}, u32[]{:S(2)}) %collective-permute-start.33) | collective-permute-done | bytes 8224 | tf_op jit(solution)/shard_map/ppermute | solution.py:72
  175.3 1.5 collective-permute-start.35
  176.8 20.0 %collective-permute-done.34.refs_3_ = bf16[320,1536]{1,0:T(8,128)(2,1)} collective-permute-done((bf16[320,1536]{1,0:T(8,128)(2,1)S(1)}, bf16[320,1536]{1,0:T(8,128)(2,1)}, u32[]{:S(2)}, u32[]{:S(2)}) %collective-permute-start.34) | collective-permute-done | bytes 983072 | tf_op jit(solution)/shard_map/ppermute | solution.py:184
  197.8 0.8 broadcast_in_dim.32.refs_5_
  198.7 4.4 %norm.3 = (bf16[5,160,512]{2,1,0:T(8,128)(2,1)}, bf16[5,160,512]{2,1,0:T(8,128)(2,1)}) custom-call(f32[2]{0:T(128)} %add_convert_fusion.refs_0_, bf16[3,320,512]{2,1,0:T(8,128)(2,1)} %conv.5.x_ref.refs_1_, bf16[1,320,512]{2,1,0:T(8,128)(2,1)} %copy-done.15, bf16[1,320,512]{2,1,0:T(8,128)(2,1)} %copy-done.16, f32[320,1]{1,0:T(8,128)} %broadcast_in_dim.31.refs_4_, ...), custom_call_target="tpu_custom_call" | custom-call | tf_op jit(solution)/shard_map/norm/pallas_call | solution.py:127
  203.0 1.5 collective-permute-start.42
  205.1 1.7 collective-permute-start.37
  206.8 17.7 %collective-permute-done.42.refs_13_ = bf16[5,160,512]{2,1,0:T(8,128)(2,1)} collective-permute-done((bf16[5,160,512]{2,1,0:T(8,128)(2,1)}, bf16[5,160,512]{2,1,0:T(8,128)(2,1)}, u32[]{:S(2)}, u32[]{:S(2)}) %collective-permute-start.42) | collective-permute-done | bytes 819232 | tf_op jit(solution)/shard_map/ppermute | solution.py:142
  224.5 13.7 %collective-permute-done.43.refs_14_ = bf16[5,160,512]{2,1,0:T(8,128)(2,1)} collective-permute-done((bf16[5,160,512]{2,1,0:T(8,128)(2,1)}, bf16[5,160,512]{2,1,0:T(8,128)(2,1)}, u32[]{:S(2)}, u32[]{:S(2)}) %collective-permute-start.43) | collective-permute-done | bytes 819232 | tf_op jit(solution)/shard_map/ppermute | solution.py:142
  238.7 0.8 slice.36
  239.7 2.0 collective-permute-start.39
  242.5 12.6 %conv.6.refs_17_ = f32[3,320,512]{2,1,0:T(8,128)} custom-call(s32[9]{0:T(128)} %pad_add_fusion.idx_ref, bf16[320,1536]{1,0:T(8,128)(2,1)} %copy-done, bf16[320,1536]{1,0:T(8,128)(2,1)} %copy-done.7, bf16[320,1536]{1,0:T(8,128)(2,1)} %copy-done.8, bf16[320,1536]{1,0:T(8,128)(2,1)} %collective-permute-done.34.refs_3_, ...), custom_call_target="tpu_custom_call" | custom-call | tf_op jit(solution)/shard_map/conv/pallas_call | solution.py:287
  255.9 0.8 copy-done.13
  256.7 13.1 %conv.7 = bf16[3,320,512]{2,1,0:T(8,128)(2,1)} custom-call(s32[9]{0:T(128)} %pad_add_fusion.idx_ref, bf16[320,1536]{1,0:T(8,128)(2,1)} %copy-done, bf16[320,1536]{1,0:T(8,128)(2,1)} %copy-done.7, bf16[320,1536]{1,0:T(8,128)(2,1)} %copy-done.8, bf16[320,1536]{1,0:T(8,128)(2,1)} %collective-permute-done.34.refs_3_, ...), custom_call_target="tpu_custom_call" | custom-call | tf_op jit(solution)/shard_map/conv/pallas_call | solution.py:287
  (133 shorter events, 9.7 us)
Async XLA Ops:
  3.6 63.2 %copy-start.1 = (bf16[320,1536]{1,0:T(8,128)(2,1)}, bf16[320,1536]{1,0:T(8,128)(2,1)S(1)}, u32[]{:S(2)}) copy-start(bf16[320,1536]{1,0:T(8,128)(2,1)S(1)} %copy.20.refs_0_) | copy-start | bytes 2949124
  3.6 64.4 %collective-permute-start.2 = (bf16[320,1536]{1,0:T(8,128)(2,1)S(1)}, bf16[320,1536]{1,0:T(8,128)(2,1)S(1)}, u32[]{:S(2)}, u32[]{:S(2)}) collective-permute-start(bf16[320,1536]{1,0:T(8,128)(2,1)S(1)} %copy.20.refs_0_), channel_id=1, source_target_pairs={{0,2},{2,4},{4,6},{6,7},{7,5},{5,3},{3,1},{1,0},{8,10},{10,12},{12... | collective-permute-start | bytes 2949128 | tf_op jit(solution)/shard_map/ppermute | solution.py:184
  6.7 61.3 %collective-permute-start.3 = (bf16[320,1536]{1,0:T(8,128)(2,1)S(1)}, bf16[320,1536]{1,0:T(8,128)(2,1)}, u32[]{:S(2)}, u32[]{:S(2)}) collective-permute-start(bf16[320,1536]{1,0:T(8,128)(2,1)S(1)} %copy.20.refs_0_), channel_id=1, source_target_pairs={{2,0},{4,2},{6,4},{7,6},{5,7},{3,5},{1,3},{0,1},{10,8},{12,10},{14... | collective-permute-start | bytes 2949128 | tf_op jit(solution)/shard_map/ppermute | solution.py:185
  7.7 60.4 %collective-permute-start.4 = (bf16[1,320,512]{2,1,0:T(8,128)(2,1)}, bf16[1,320,512]{2,1,0:T(8,128)(2,1)S(1)}, u32[]{:S(2)}, u32[]{:S(2)}) collective-permute-start(bf16[1,320,512]{2,1,0:T(8,128)(2,1)} %get-tuple-element.24), channel_id=1, source_target_pairs={{0,1},{1,2},{2,3},{3,4},{4,5},{5,6},{6,7},{8,9},{9,10},{10,11},{11... | collective-permute-start | bytes 983048 | tf_op jit(solution)/shard_map/ppermute | solution.py:109
  11.5 56.5 %collective-permute-start.5 = (bf16[1,320,512]{2,1,0:T(8,128)(2,1)}, bf16[1,320,512]{2,1,0:T(8,128)(2,1)}, u32[]{:S(2)}, u32[]{:S(2)}) collective-permute-start(bf16[1,320,512]{2,1,0:T(8,128)(2,1)} %get-tuple-element.23), channel_id=1, source_target_pairs={{1,0},{2,1},{3,2},{4,3},{5,4},{6,5},{7,6},{9,8},{10,9},{11,10},{12... | collective-permute-start | bytes 983048 | tf_op jit(solution)/shard_map/ppermute | solution.py:110
  15.9 15.1 %collective-permute-start.10 = (f32[2,8,128]{2,1,0:T(8,128)}, f32[2,8,128]{2,1,0:T(8,128)S(1)}, u32[]{:S(2)}, u32[]{:S(2)}) collective-permute-start(f32[2,8,128]{2,1,0:T(8,128)} %stats.2.refs_6_), channel_id=1, source_target_pairs={{0,5},{1,4},{2,7},{3,6},{4,1},{5,0},{6,3},{7,2},{8,13},{9,12},{10,... | collective-permute-start | bytes 24584 | tf_op jit(solution)/shard_map/ppermute | solution.py:72
  31.0 37.0 %copy-start.17 = (f32[2,8,128]{2,1,0:T(8,128)}, f32[2,8,128]{2,1,0:T(8,128)S(1)}, u32[]{:S(2)}) copy-start(f32[2,8,128]{2,1,0:T(8,128)S(1)} %collective-permute-done.10.refs_11_) | copy-start | bytes 24580
  31.0 11.5 %collective-permute-start.11 = (f32[2,8,128]{2,1,0:T(8,128)}, f32[2,8,128]{2,1,0:T(8,128)S(1)}, u32[]{:S(2)}, u32[]{:S(2)}) collective-permute-start(f32[2,8,128]{2,1,0:T(8,128)} %stats.2.refs_6_), channel_id=1, source_target_pairs={{0,6},{1,7},{2,4},{3,5},{4,2},{5,3},{6,0},{7,1},{8,14},{9,15},{10,... | collective-permute-start | bytes 24584 | tf_op jit(solution)/shard_map/ppermute | solution.py:72
  42.5 25.5 %copy-start.19 = (f32[2,8,128]{2,1,0:T(8,128)}, f32[2,8,128]{2,1,0:T(8,128)S(1)}, u32[]{:S(2)}) copy-start(f32[2,8,128]{2,1,0:T(8,128)S(1)} %collective-permute-done.11.refs_12_) | copy-start | bytes 24580
  42.5 6.6 %collective-permute-start.12 = (f32[2,8,128]{2,1,0:T(8,128)}, f32[2,8,128]{2,1,0:T(8,128)S(1)}, u32[]{:S(2)}, u32[]{:S(2)}) collective-permute-start(f32[2,8,128]{2,1,0:T(8,128)} %stats.2.refs_6_), channel_id=1, source_target_pairs={{0,7},{1,6},{2,5},{3,4},{4,3},{5,2},{6,1},{7,0},{8,15},{9,14},{10,... | collective-permute-start | bytes 24584 | tf_op jit(solution)/shard_map/ppermute | solution.py:72
  49.1 4.8 %collective-permute-start.6 = (f32[2,8,128]{2,1,0:T(8,128)}, f32[2,8,128]{2,1,0:T(8,128)S(1)}, u32[]{:S(2)}, u32[]{:S(2)}) collective-permute-start(f32[2,8,128]{2,1,0:T(8,128)} %stats.2.refs_6_), channel_id=1, source_target_pairs={{0,1},{1,0},{2,3},{3,2},{4,5},{5,4},{6,7},{7,6},{8,9},{9,8},{10,11... | collective-permute-start | bytes 24584 | tf_op jit(solution)/shard_map/ppermute | solution.py:72
  53.9 3.9 %collective-permute-start.7 = (f32[2,8,128]{2,1,0:T(8,128)}, f32[2,8,128]{2,1,0:T(8,128)S(1)}, u32[]{:S(2)}, u32[]{:S(2)}) collective-permute-start(f32[2,8,128]{2,1,0:T(8,128)} %stats.2.refs_6_), channel_id=1, source_target_pairs={{0,2},{1,3},{2,0},{3,1},{4,6},{5,7},{6,4},{7,5},{8,10},{9,11},{10,... | collective-permute-start | bytes 24584 | tf_op jit(solution)/shard_map/ppermute | solution.py:72
  57.8 4.8 %collective-permute-start.8 = (f32[2,8,128]{2,1,0:T(8,128)}, f32[2,8,128]{2,1,0:T(8,128)S(1)}, u32[]{:S(2)}, u32[]{:S(2)}) collective-permute-start(f32[2,8,128]{2,1,0:T(8,128)} %stats.2.refs_6_), channel_id=1, source_target_pairs={{0,3},{1,2},{2,1},{3,0},{4,7},{5,6},{6,5},{7,4},{8,11},{9,10},{10,... | collective-permute-start | bytes 24584 | tf_op jit(solution)/shard_map/ppermute | solution.py:72
  62.5 5.5 %collective-permute-start.9 = (f32[2,8,128]{2,1,0:T(8,128)}, f32[2,8,128]{2,1,0:T(8,128)S(1)}, u32[]{:S(2)}, u32[]{:S(2)}) collective-permute-start(f32[2,8,128]{2,1,0:T(8,128)} %stats.2.refs_6_), channel_id=1, source_target_pairs={{0,4},{1,5},{2,6},{3,7},{4,0},{5,1},{6,2},{7,3},{8,12},{9,13},{10,... | collective-permute-start | bytes 24584 | tf_op jit(solution)/shard_map/ppermute | solution.py:72
  68.1 23.9 %copy-start.9 = (bf16[320,1536]{1,0:T(8,128)(2,1)}, bf16[320,1536]{1,0:T(8,128)(2,1)S(1)}, u32[]{:S(2)}) copy-start(bf16[320,1536]{1,0:T(8,128)(2,1)S(1)} %collective-permute-done.2.refs_1_) | copy-start | bytes 2949124
  68.1 21.9 %collective-permute-start.13 = (bf16[320,1536]{1,0:T(8,128)(2,1)S(1)}, bf16[320,1536]{1,0:T(8,128)(2,1)S(1)}, u32[]{:S(2)}, u32[]{:S(2)}) collective-permute-start(bf16[320,1536]{1,0:T(8,128)(2,1)S(1)} %collective-permute-done.2.refs_1_), channel_id=1, source_target_pairs={{0,2},{2,4},{4,6},{6,7},{7,5},{5,3},{3,1},{1,0},{8,10},{10,12},{12... | collective-permute-start | bytes 2949128 | tf_op jit(solution)/shard_map/ppermute | solution.py:184
  70.2 21.8 %collective-permute-start.14 = (bf16[320,1536]{1,0:T(8,128)(2,1)}, bf16[320,1536]{1,0:T(8,128)(2,1)}, u32[]{:S(2)}, u32[]{:S(2)}) collective-permute-start(bf16[320,1536]{1,0:T(8,128)(2,1)} %collective-permute-done.3.refs_2_), channel_id=1, source_target_pairs={{2,0},{4,2},{6,4},{7,6},{5,7},{3,5},{1,3},{0,1},{10,8},{12,10},{14... | collective-permute-start | bytes 2949128 | tf_op jit(solution)/shard_map/ppermute | solution.py:185
  76.8 21.4 %collective-permute-start.21 = (bf16[5,160,512]{2,1,0:T(8,128)(2,1)}, bf16[5,160,512]{2,1,0:T(8,128)(2,1)}, u32[]{:S(2)}, u32[]{:S(2)}) collective-permute-start(bf16[5,160,512]{2,1,0:T(8,128)(2,1)} %get-tuple-element.15.refs_7_.refs_9_), channel_id=1, source_target_pairs={{0,16},{8,24},{16,0},{24,8},{1,17},{9,25},{17,1},{25,9},{2,18},{10... | collective-permute-start | bytes 2457608 | tf_op jit(solution)/shard_map/ppermute | solution.py:142
  78.3 28.9 %collective-permute-start.22 = (bf16[5,160,512]{2,1,0:T(8,128)(2,1)}, bf16[5,160,512]{2,1,0:T(8,128)(2,1)}, u32[]{:S(2)}, u32[]{:S(2)}) collective-permute-start(bf16[5,160,512]{2,1,0:T(8,128)(2,1)} %get-tuple-element.16.refs_8_.refs_10_), channel_id=1, source_target_pairs={{0,16},{8,24},{16,0},{24,8},{1,17},{9,25},{17,1},{25,9},{2,18},{10... | collective-permute-start | bytes 2457608 | tf_op jit(solution)/shard_map/ppermute | solution.py:142
  89.9 21.1 %copy-start.10 = (bf16[320,1536]{1,0:T(8,128)(2,1)}, bf16[320,1536]{1,0:T(8,128)(2,1)S(1)}, u32[]{:S(2)}) copy-start(bf16[320,1536]{1,0:T(8,128)(2,1)S(1)} %collective-permute-done.13.refs_3_) | copy-start | bytes 2949124
  90.0 17.2 %collective-permute-start.15 = (bf16[320,1536]{1,0:T(8,128)(2,1)S(1)}, bf16[320,1536]{1,0:T(8,128)(2,1)S(1)}, u32[]{:S(2)}, u32[]{:S(2)}) collective-permute-start(bf16[320,1536]{1,0:T(8,128)(2,1)S(1)} %collective-permute-done.13.refs_3_), channel_id=1, source_target_pairs={{0,2},{2,4},{4,6},{6,7},{7,5},{5,3},{3,1},{1,0},{8,10},{10,12},{12... | collective-permute-start | bytes 2949128 | tf_op jit(solution)/shard_map/ppermute | solution.py:184
  92.0 16.5 %collective-permute-start.16 = (bf16[320,1536]{1,0:T(8,128)(2,1)}, bf16[320,1536]{1,0:T(8,128)(2,1)S(1)}, u32[]{:S(2)}, u32[]{:S(2)}) collective-permute-start(bf16[320,1536]{1,0:T(8,128)(2,1)} %collective-permute-done.14.refs_4_), channel_id=1, source_target_pairs={{2,0},{4,2},{6,4},{7,6},{5,7},{3,5},{1,3},{0,1},{10,8},{12,10},{14... | collective-permute-start | bytes 2949128 | tf_op jit(solution)/shard_map/ppermute | solution.py:185
  92.0 19.1 %collective-permute-start.19 = (bf16[5,160,512]{2,1,0:T(8,128)(2,1)}, bf16[5,160,512]{2,1,0:T(8,128)(2,1)S(1)}, u32[]{:S(2)}, u32[]{:S(2)}) collective-permute-start(bf16[5,160,512]{2,1,0:T(8,128)(2,1)} %get-tuple-element.15.refs_7_.refs_9_), channel_id=1, source_target_pairs={{0,8},{8,0},{16,24},{24,16},{1,9},{9,1},{17,25},{25,17},{2,10},{10... | collective-permute-start | bytes 2457608 | tf_op jit(solution)/shard_map/ppermute | solution.py:142
  98.2 15.6 %collective-permute-start.20 = (bf16[5,160,512]{2,1,0:T(8,128)(2,1)}, bf16[5,160,512]{2,1,0:T(8,128)(2,1)}, u32[]{:S(2)}, u32[]{:S(2)}) collective-permute-start(bf16[5,160,512]{2,1,0:T(8,128)(2,1)} %get-tuple-element.16.refs_8_.refs_10_), channel_id=1, source_target_pairs={{0,8},{8,0},{16,24},{24,16},{1,9},{9,1},{17,25},{25,17},{2,10},{10... | collective-permute-start | bytes 2457608 | tf_op jit(solution)/shard_map/ppermute | solution.py:142
  107.2 8.5 %collective-permute-start.23 = (bf16[5,160,512]{2,1,0:T(8,128)(2,1)}, bf16[5,160,512]{2,1,0:T(8,128)(2,1)}, u32[]{:S(2)}, u32[]{:S(2)}) collective-permute-start(bf16[5,160,512]{2,1,0:T(8,128)(2,1)} %collective-permute-done.21.refs_13_), channel_id=1, source_target_pairs={{0,8},{8,0},{16,24},{24,16},{1,9},{9,1},{17,25},{25,17},{2,10},{10... | collective-permute-start | bytes 2457608 | tf_op jit(solution)/shard_map/ppermute | solution.py:142
  107.2 22.7 %collective-permute-start.24 = (bf16[5,160,512]{2,1,0:T(8,128)(2,1)}, bf16[5,160,512]{2,1,0:T(8,128)(2,1)}, u32[]{:S(2)}, u32[]{:S(2)}) collective-permute-start(bf16[5,160,512]{2,1,0:T(8,128)(2,1)} %collective-permute-done.22.refs_14_), channel_id=1, source_target_pairs={{0,8},{8,0},{16,24},{24,16},{1,9},{9,1},{17,25},{25,17},{2,10},{10... | collective-permute-start | bytes 2457608 | tf_op jit(solution)/shard_map/ppermute | solution.py:142
  108.5 21.4 %collective-permute-start.17 = (bf16[160,1536]{1,0:T(8,128)(2,1)}, bf16[160,1536]{1,0:T(8,128)(2,1)}, u32[]{:S(2)}, u32[]{:S(2)}) collective-permute-start(bf16[160,1536]{1,0:T(8,128)(2,1)} %slice.32), channel_id=1, source_target_pairs={{0,2},{2,4},{4,6},{6,7},{7,5},{5,3},{3,1},{1,0},{8,10},{10,12},{12... | collective-permute-start | bytes 1474568 | tf_op jit(solution)/shard_map/ppermute | solution.py:184
  112.0 18.0 %collective-permute-start.18 = (bf16[160,1536]{1,0:T(8,128)(2,1)}, bf16[160,1536]{1,0:T(8,128)(2,1)}, u32[]{:S(2)}, u32[]{:S(2)}) collective-permute-start(bf16[160,1536]{1,0:T(8,128)(2,1)} %slice.33), channel_id=1, source_target_pairs={{2,0},{4,2},{6,4},{7,6},{5,7},{3,5},{1,3},{0,1},{10,8},{12,10},{14... | collective-permute-start | bytes 1474568 | tf_op jit(solution)/shard_map/ppermute | solution.py:185
  113.9 41.2 %collective-permute-start = (bf16[320,1536]{1,0:T(8,128)(2,1)S(1)}, bf16[320,1536]{1,0:T(8,128)(2,1)S(1)}, u32[]{:S(2)}, u32[]{:S(2)}) collective-permute-start(bf16[320,1536]{1,0:T(8,128)(2,1)S(1)} %copy.25.refs_0_), channel_id=1, source_target_pairs={{0,2},{2,4},{4,6},{6,7},{7,5},{5,3},{3,1},{1,0},{8,10},{10,12},{12... | collective-permute-start | bytes 2949128 | tf_op jit(solution)/shard_map/ppermute | solution.py:184
  115.7 41.0 %collective-permute-start.1 = (bf16[320,1536]{1,0:T(8,128)(2,1)S(1)}, bf16[320,1536]{1,0:T(8,128)(2,1)S(1)}, u32[]{:S(2)}, u32[]{:S(2)}) collective-permute-start(bf16[320,1536]{1,0:T(8,128)(2,1)S(1)} %copy.25.refs_0_), channel_id=1, source_target_pairs={{2,0},{4,2},{6,4},{7,6},{5,7},{3,5},{1,3},{0,1},{10,8},{12,10},{14... | collective-permute-start | bytes 2949128 | tf_op jit(solution)/shard_map/ppermute | solution.py:185
  143.1 54.0 %copy-start.34 = (f32[320]{0:T(512)S(1)}, f32[320]{0:T(512)}, u32[]{:S(2)}) copy-start(f32[320]{0:T(512)} %param.15) | copy-start | bytes 3844
  143.1 54.8 %copy-start.35 = (f32[320]{0:T(512)S(1)}, f32[320]{0:T(512)}, u32[]{:S(2)}) copy-start(f32[320]{0:T(512)} %param.16) | copy-start | bytes 3844
  145.1 29.6 %collective-permute-start.25 = (bf16[1,320,512]{2,1,0:T(8,128)(2,1)}, bf16[1,320,512]{2,1,0:T(8,128)(2,1)S(1)}, u32[]{:S(2)}, u32[]{:S(2)}) collective-permute-start(bf16[1,320,512]{2,1,0:T(8,128)(2,1)} %get-tuple-element.22), channel_id=1, source_target_pairs={{0,1},{1,2},{2,3},{3,4},{4,5},{5,6},{6,7},{8,9},{9,10},{10,11},{11... | collective-permute-start | bytes 983048 | tf_op jit(solution)/shard_map/ppermute | solution.py:109
  147.6 27.1 %collective-permute-start.26 = (bf16[1,320,512]{2,1,0:T(8,128)(2,1)}, bf16[1,320,512]{2,1,0:T(8,128)(2,1)S(1)}, u32[]{:S(2)}, u32[]{:S(2)}) collective-permute-start(bf16[1,320,512]{2,1,0:T(8,128)(2,1)} %get-tuple-element.21), channel_id=1, source_target_pairs={{1,0},{2,1},{3,2},{4,3},{5,4},{6,5},{7,6},{9,8},{10,9},{11,10},{12... | collective-permute-start | bytes 983048 | tf_op jit(solution)/shard_map/ppermute | solution.py:110
  152.1 9.2 %collective-permute-start.27 = (f32[2,8,128]{2,1,0:T(8,128)}, f32[2,8,128]{2,1,0:T(8,128)S(1)}, u32[]{:S(2)}, u32[]{:S(2)}) collective-permute-start(f32[2,8,128]{2,1,0:T(8,128)} %stats.3.refs_6_), channel_id=1, source_target_pairs={{0,1},{1,0},{2,3},{3,2},{4,5},{5,4},{6,7},{7,6},{8,9},{9,8},{10,11... | collective-permute-start | bytes 24584 | tf_op jit(solution)/shard_map/ppermute | solution.py:72
  155.1 84.4 %copy-start.7 = (bf16[320,1536]{1,0:T(8,128)(2,1)}, bf16[320,1536]{1,0:T(8,128)(2,1)S(1)}, u32[]{:S(2)}) copy-start(bf16[320,1536]{1,0:T(8,128)(2,1)S(1)} %collective-permute-done.refs_1_) | copy-start | bytes 2949124
  155.1 10.1 %collective-permute-start.28 = (f32[2,8,128]{2,1,0:T(8,128)}, f32[2,8,128]{2,1,0:T(8,128)S(1)}, u32[]{:S(2)}, u32[]{:S(2)}) collective-permute-start(f32[2,8,128]{2,1,0:T(8,128)} %stats.3.refs_6_), channel_id=1, source_target_pairs={{0,2},{1,3},{2,0},{3,1},{4,6},{5,7},{6,4},{7,5},{8,10},{9,11},{10,... | collective-permute-start | bytes 24584 | tf_op jit(solution)/shard_map/ppermute | solution.py:72
  156.7 82.8 %copy-start.8 = (bf16[320,1536]{1,0:T(8,128)(2,1)}, bf16[320,1536]{1,0:T(8,128)(2,1)S(1)}, u32[]{:S(2)}) copy-start(bf16[320,1536]{1,0:T(8,128)(2,1)S(1)} %collective-permute-done.1.refs_2_) | copy-start | bytes 2949124
  156.7 9.5 %collective-permute-start.29 = (f32[2,8,128]{2,1,0:T(8,128)}, f32[2,8,128]{2,1,0:T(8,128)S(1)}, u32[]{:S(2)}, u32[]{:S(2)}) collective-permute-start(f32[2,8,128]{2,1,0:T(8,128)} %stats.3.refs_6_), channel_id=1, source_target_pairs={{0,3},{1,2},{2,1},{3,0},{4,7},{5,6},{6,5},{7,4},{8,11},{9,10},{10,... | collective-permute-start | bytes 24584 | tf_op jit(solution)/shard_map/ppermute | solution.py:72
  161.3 37.3 %copy-start.18 = (f32[2,8,128]{2,1,0:T(8,128)}, f32[2,8,128]{2,1,0:T(8,128)S(1)}, u32[]{:S(2)}) copy-start(f32[2,8,128]{2,1,0:T(8,128)S(1)} %collective-permute-done.27.refs_7_) | copy-start | bytes 24580
  161.3 6.7 %collective-permute-start.30 = (f32[2,8,128]{2,1,0:T(8,128)}, f32[2,8,128]{2,1,0:T(8,128)S(1)}, u32[]{:S(2)}, u32[]{:S(2)}) collective-permute-start(f32[2,8,128]{2,1,0:T(8,128)} %stats.3.refs_6_), channel_id=1, source_target_pairs={{0,4},{1,5},{2,6},{3,7},{4,0},{5,1},{6,2},{7,3},{8,12},{9,13},{10,... | collective-permute-start | bytes 24584 | tf_op jit(solution)/shard_map/ppermute | solution.py:72
  165.2 33.4 %copy-start.20 = (f32[2,8,128]{2,1,0:T(8,128)}, f32[2,8,128]{2,1,0:T(8,128)S(1)}, u32[]{:S(2)}) copy-start(f32[2,8,128]{2,1,0:T(8,128)S(1)} %collective-permute-done.28.refs_8_) | copy-start | bytes 24580
  165.2 5.7 %collective-permute-start.31 = (f32[2,8,128]{2,1,0:T(8,128)}, f32[2,8,128]{2,1,0:T(8,128)S(1)}, u32[]{:S(2)}, u32[]{:S(2)}) collective-permute-start(f32[2,8,128]{2,1,0:T(8,128)} %stats.3.refs_6_), channel_id=1, source_target_pairs={{0,5},{1,4},{2,7},{3,6},{4,1},{5,0},{6,3},{7,2},{8,13},{9,12},{10,... | collective-permute-start | bytes 24584 | tf_op jit(solution)/shard_map/ppermute | solution.py:72
  166.1 32.5 %copy-start.22 = (f32[2,8,128]{2,1,0:T(8,128)}, f32[2,8,128]{2,1,0:T(8,128)S(1)}, u32[]{:S(2)}) copy-start(f32[2,8,128]{2,1,0:T(8,128)S(1)} %collective-permute-done.29.refs_9_) | copy-start | bytes 24580
  166.1 5.7 %collective-permute-start.32 = (f32[2,8,128]{2,1,0:T(8,128)}, f32[2,8,128]{2,1,0:T(8,128)S(1)}, u32[]{:S(2)}, u32[]{:S(2)}) collective-permute-start(f32[2,8,128]{2,1,0:T(8,128)} %stats.3.refs_6_), channel_id=1, source_target_pairs={{0,6},{1,7},{2,4},{3,5},{4,2},{5,3},{6,0},{7,1},{8,14},{9,15},{10,... | collective-permute-start | bytes 24584 | tf_op jit(solution)/shard_map/ppermute | solution.py:72
  168.1 30.6 %copy-start.24 = (f32[2,8,128]{2,1,0:T(8,128)}, f32[2,8,128]{2,1,0:T(8,128)S(1)}, u32[]{:S(2)}) copy-start(f32[2,8,128]{2,1,0:T(8,128)S(1)} %collective-permute-done.30.refs_10_) | copy-start | bytes 24580
  168.1 6.6 %collective-permute-start.33 = (f32[2,8,128]{2,1,0:T(8,128)}, f32[2,8,128]{2,1,0:T(8,128)S(1)}, u32[]{:S(2)}, u32[]{:S(2)}) collective-permute-start(f32[2,8,128]{2,1,0:T(8,128)} %stats.3.refs_6_), channel_id=1, source_target_pairs={{0,7},{1,6},{2,5},{3,4},{4,3},{5,2},{6,1},{7,0},{8,15},{9,14},{10,... | collective-permute-start | bytes 24584 | tf_op jit(solution)/shard_map/ppermute | solution.py:72
  170.9 27.7 %copy-start.26 = (f32[2,8,128]{2,1,0:T(8,128)}, f32[2,8,128]{2,1,0:T(8,128)S(1)}, u32[]{:S(2)}) copy-start(f32[2,8,128]{2,1,0:T(8,128)S(1)} %collective-permute-done.31.refs_11_) | copy-start | bytes 24580
  171.8 26.8 %copy-start.28 = (f32[2,8,128]{2,1,0:T(8,128)}, f32[2,8,128]{2,1,0:T(8,128)S(1)}, u32[]{:S(2)}) copy-start(f32[2,8,128]{2,1,0:T(8,128)S(1)} %collective-permute-done.32.refs_12_) | copy-start | bytes 24580
  174.7 24.0 %copy-start.30 = (f32[2,8,128]{2,1,0:T(8,128)}, f32[2,8,128]{2,1,0:T(8,128)S(1)}, u32[]{:S(2)}) copy-start(f32[2,8,128]{2,1,0:T(8,128)S(1)} %collective-permute-done.33.refs_13_) | copy-start | bytes 24580
  174.7 24.0 %copy-start.15 = (bf16[1,320,512]{2,1,0:T(8,128)(2,1)}, bf16[1,320,512]{2,1,0:T(8,128)(2,1)S(1)}, u32[]{:S(2)}) copy-start(bf16[1,320,512]{2,1,0:T(8,128)(2,1)S(1)} %collective-permute-done.25.refs_2_) | copy-start | bytes 983044
  174.7 22.1 %collective-permute-start.34 = (bf16[320,1536]{1,0:T(8,128)(2,1)S(1)}, bf16[320,1536]{1,0:T(8,128)(2,1)}, u32[]{:S(2)}, u32[]{:S(2)}) collective-permute-start(bf16[320,1536]{1,0:T(8,128)(2,1)S(1)} %collective-permute-done.refs_1_), channel_id=1, source_target_pairs={{0,2},{2,4},{4,6},{6,7},{7,5},{5,3},{3,1},{1,0},{8,10},{10,12},{12... | collective-permute-start | bytes 2949128 | tf_op jit(solution)/shard_map/ppermute | solution.py:184
  175.3 29.8 %collective-permute-start.35 = (bf16[320,1536]{1,0:T(8,128)(2,1)S(1)}, bf16[320,1536]{1,0:T(8,128)(2,1)}, u32[]{:S(2)}, u32[]{:S(2)}) collective-permute-start(bf16[320,1536]{1,0:T(8,128)(2,1)S(1)} %collective-permute-done.1.refs_2_), channel_id=1, source_target_pairs={{2,0},{4,2},{6,4},{7,6},{5,7},{3,5},{1,3},{0,1},{10,8},{12,10},{14... | collective-permute-start | bytes 2949128 | tf_op jit(solution)/shard_map/ppermute | solution.py:185
  196.8 41.4 %collective-permute-start.36 = (bf16[320,1536]{1,0:T(8,128)(2,1)}, bf16[320,1536]{1,0:T(8,128)(2,1)S(1)}, u32[]{:S(2)}, u32[]{:S(2)}) collective-permute-start(bf16[320,1536]{1,0:T(8,128)(2,1)} %collective-permute-done.34.refs_3_), channel_id=1, source_target_pairs={{0,2},{2,4},{4,6},{6,7},{7,5},{5,3},{3,1},{1,0},{8,10},{10,12},{12... | collective-permute-start | bytes 2949128 | tf_op jit(solution)/shard_map/ppermute | solution.py:184
  203.0 38.7 %copy-start.36 = (f32[320]{0:T(512)S(1)}, f32[320]{0:T(512)}, u32[]{:S(2)}) copy-start(f32[320]{0:T(512)} %param.18) | copy-start | bytes 3844
  203.0 21.4 %collective-permute-start.42 = (bf16[5,160,512]{2,1,0:T(8,128)(2,1)}, bf16[5,160,512]{2,1,0:T(8,128)(2,1)}, u32[]{:S(2)}, u32[]{:S(2)}) collective-permute-start(bf16[5,160,512]{2,1,0:T(8,128)(2,1)} %get-tuple-element.19.refs_7_.refs_9_), channel_id=1, source_target_pairs={{0,16},{8,24},{16,0},{24,8},{1,17},{9,25},{17,1},{25,9},{2,18},{10... | collective-permute-start | bytes 2457608 | tf_op jit(solution)/shard_map/ppermute | solution.py:142
  204.6 33.6 %collective-permute-start.43 = (bf16[5,160,512]{2,1,0:T(8,128)(2,1)}, bf16[5,160,512]{2,1,0:T(8,128)(2,1)}, u32[]{:S(2)}, u32[]{:S(2)}) collective-permute-start(bf16[5,160,512]{2,1,0:T(8,128)(2,1)} %get-tuple-element.20.refs_8_.refs_10_), channel_id=1, source_target_pairs={{0,16},{8,24},{16,0},{24,8},{1,17},{9,25},{17,1},{25,9},{2,18},{10... | collective-permute-start | bytes 2457608 | tf_op jit(solution)/shard_map/ppermute | solution.py:142
  205.1 34.4 %collective-permute-start.37 = (bf16[320,1536]{1,0:T(8,128)(2,1)}, bf16[320,1536]{1,0:T(8,128)(2,1)S(1)}, u32[]{:S(2)}, u32[]{:S(2)}) collective-permute-start(bf16[320,1536]{1,0:T(8,128)(2,1)} %collective-permute-done.35.refs_4_), channel_id=1, source_target_pairs={{2,0},{4,2},{6,4},{7,6},{5,7},{3,5},{1,3},{0,1},{10,8},{12,10},{14... | collective-permute-start | bytes 2949128 | tf_op jit(solution)/shard_map/ppermute | solution.py:185
  206.8 32.9 %collective-permute-start.40 = (bf16[5,160,512]{2,1,0:T(8,128)(2,1)}, bf16[5,160,512]{2,1,0:T(8,128)(2,1)}, u32[]{:S(2)}, u32[]{:S(2)}) collective-permute-start(bf16[5,160,512]{2,1,0:T(8,128)(2,1)} %get-tuple-element.19.refs_7_.refs_9_), channel_id=1, source_target_pairs={{0,8},{8,0},{16,24},{24,16},{1,9},{9,1},{17,25},{25,17},{2,10},{10... | collective-permute-start | bytes 2457608 | tf_op jit(solution)/shard_map/ppermute | solution.py:142
  224.5 18.0 %collective-permute-start.41 = (bf16[5,160,512]{2,1,0:T(8,128)(2,1)}, bf16[5,160,512]{2,1,0:T(8,128)(2,1)}, u32[]{:S(2)}, u32[]{:S(2)}) collective-permute-start(bf16[5,160,512]{2,1,0:T(8,128)(2,1)} %get-tuple-element.20.refs_8_.refs_10_), channel_id=1, source_target_pairs={{0,8},{8,0},{16,24},{24,16},{1,9},{9,1},{17,25},{25,17},{2,10},{10... | collective-permute-start | bytes 2457608 | tf_op jit(solution)/shard_map/ppermute | solution.py:142
  238.2 17.0 %collective-permute-start.44 = (bf16[5,160,512]{2,1,0:T(8,128)(2,1)}, bf16[5,160,512]{2,1,0:T(8,128)(2,1)}, u32[]{:S(2)}, u32[]{:S(2)}) collective-permute-start(bf16[5,160,512]{2,1,0:T(8,128)(2,1)} %collective-permute-done.42.refs_13_), channel_id=1, source_target_pairs={{0,8},{8,0},{16,24},{24,16},{1,9},{9,1},{17,25},{25,17},{2,10},{10... | collective-permute-start | bytes 2457608 | tf_op jit(solution)/shard_map/ppermute | solution.py:142
  238.2 17.0 %collective-permute-start.45 = (bf16[5,160,512]{2,1,0:T(8,128)(2,1)}, bf16[5,160,512]{2,1,0:T(8,128)(2,1)}, u32[]{:S(2)}, u32[]{:S(2)}) collective-permute-start(bf16[5,160,512]{2,1,0:T(8,128)(2,1)} %collective-permute-done.43.refs_14_), channel_id=1, source_target_pairs={{0,8},{8,0},{16,24},{24,16},{1,9},{9,1},{17,25},{25,17},{2,10},{10... | collective-permute-start | bytes 2457608 | tf_op jit(solution)/shard_map/ppermute | solution.py:142
  239.5 15.6 %collective-permute-start.38 = (bf16[160,1536]{1,0:T(8,128)(2,1)}, bf16[160,1536]{1,0:T(8,128)(2,1)S(1)}, u32[]{:S(2)}, u32[]{:S(2)}) collective-permute-start(bf16[160,1536]{1,0:T(8,128)(2,1)} %slice.36), channel_id=1, source_target_pairs={{0,2},{2,4},{4,6},{6,7},{7,5},{5,3},{3,1},{1,0},{8,10},{10,12},{12... | collective-permute-start | bytes 1474568 | tf_op jit(solution)/shard_map/ppermute | solution.py:184
  239.7 15.5 %collective-permute-start.39 = (bf16[160,1536]{1,0:T(8,128)(2,1)S(1)}, bf16[160,1536]{1,0:T(8,128)(2,1)S(1)}, u32[]{:S(2)}, u32[]{:S(2)}) collective-permute-start(bf16[160,1536]{1,0:T(8,128)(2,1)S(1)} %slice.37), channel_id=1, source_target_pairs={{2,0},{4,2},{6,4},{7,6},{5,7},{3,5},{1,3},{0,1},{10,8},{12,10},{14... | collective-permute-start | bytes 1474568 | tf_op jit(solution)/shard_map/ppermute | solution.py:185
  (20 other events, 119.1 us)

commit v2 on v1

v2 whole, which is shorter than its diff:
```python
import jax
import jax.numpy as jnp
from jax import lax
from jax.experimental import pallas as pl
from jax.experimental.pallas import tpu as pltpu
from jax.sharding import PartitionSpec as P


C = 1280
GROUPS = 32
WIDTH = 32
GROUP_SIZE = C // GROUPS
TAPS = 3
EPS = 1e-05
VMEM_LIMIT = 60 * 1024 * 1024


def params(**extra):
    return pltpu.CompilerParams(vmem_limit_bytes=VMEM_LIMIT, **extra)


def xor_pairs(count, bit):
    return [(i, i ^ bit) for i in range(count)]


def image_select(lanes, images=128):
    lane = lax.broadcasted_iota(jnp.int32, (lanes, images), 0) // WIDTH
    return (lane == lax.broadcasted_iota(jnp.int32, (lanes, images), 1)).astype(jnp.float32)


def image_sum(value, select):
    return jnp.dot(value, select, precision=lax.Precision.HIGHEST, preferred_element_type=jnp.float32)


def image_spread(value, select):
    return lax.dot_general(
        value, select, (((1,), (1,)), ((), ())), precision=lax.Precision.HIGHEST, preferred_element_type=jnp.float32
    )


def stats_into(x_ref, out_ref, total_ref):
    rows, chans, lanes = x_ref.shape
    groups = chans // GROUP_SIZE
    count = rows * GROUP_SIZE * WIDTH
    select = image_select(lanes)
    spans = [slice(g * GROUP_SIZE, (g + 1) * GROUP_SIZE) for g in range(groups)]
    for g in range(groups):
        part = x_ref[:, spans[g], :].astype(jnp.float32)
        total_ref[g : g + 1, :] = jnp.sum(jnp.sum(part, axis=0), axis=0, keepdims=True)
    mean = image_sum(total_ref[...], select) / count
    out_ref[0] = mean
    wide = image_spread(mean, select)
    for g in range(groups):
        off = x_ref[:, spans[g], :].astype(jnp.float32) - wide[None, g : g + 1, :]
        total_ref[g : g + 1, :] = jnp.sum(jnp.sum(off * off, axis=0), axis=0, keepdims=True)
    out_ref[1] = image_sum(total_ref[...], select)


def edge_shapes(x_shape):
    _, chans, lanes = x_shape
    edge = jax.ShapeDtypeStruct((1, chans, lanes), jnp.bfloat16)
    return [edge, edge, jax.ShapeDtypeStruct((2, chans // GROUP_SIZE, 128), jnp.float32)]


def summary_of(x):
    def body(x_ref, top_ref, bottom_ref, stats_ref, total_ref):
        rows = x_ref.shape[0]
        top_ref[0] = x_ref[0]
        bottom_ref[0] = x_ref[rows - 1]
        stats_into(x_ref, stats_ref, total_ref)

    return pl.pallas_call(
        body,
        out_shape=edge_shapes(x.shape),
        scratch_shapes=[pltpu.VMEM((x.shape[1] // GROUP_SIZE, x.shape[2]), jnp.float32)],
        compiler_params=params(),
        name="stats",
    )(x)


def surroundings(summary):
    n_row = lax.axis_size("row")
    top, bottom, stats = summary
    above = lax.ppermute(bottom, "row", [(i, i + 1) for i in range(n_row - 1)])
    below = lax.ppermute(top, "row", [(i + 1, i) for i in range(n_row - 1)])
    every = [stats]
    for k in range(1, n_row):
        every.append(lax.ppermute(stats, "row", xor_pairs(n_row, k)))
    return (above, below), every


def norm_body(count, n_row, column, flag_ref, x_ref, above_ref, below_ref, columns_ref, *refs):
    stats_refs = refs[:n_row]
    out_refs = refs[n_row:]
    rows, chans, lanes = x_ref.shape
    groups = chans // GROUP_SIZE
    width = out_refs[0].shape[1]
    select = image_select(lanes)
    center = sum(ref[0] for ref in stats_refs) / n_row
    square = sum(ref[1] for ref in stats_refs) + count * sum(jnp.square(ref[0] - center) for ref in stats_refs)
    scale = lax.rsqrt(square / (count * n_row) + EPS)
    wide_center = image_spread(center, select)
    wide_scale = image_spread(scale, select)
    for g in range(groups):
        span = slice(g * GROUP_SIZE, (g + 1) * GROUP_SIZE)
        out_ref = out_refs[g * GROUP_SIZE // width]
        start = g * GROUP_SIZE % width
        mean = wide_center[g : g + 1, :]
        inv = wide_scale[g : g + 1, :]
        gain = columns_ref[span, column : column + 1]
        shift = columns_ref[span, column + 1 : column + 2]

        def act(value):
            v = (value.astype(jnp.float32) - mean) * inv * gain + shift
            return v / (1.0 + jnp.exp(-v))

        here = slice(start, start + GROUP_SIZE)
        out_ref[0, here, :] = (act(above_ref[0, span, :]) * flag_ref[0]).astype(jnp.bfloat16)
        for r in range(rows):
            out_ref[r + 1, here, :] = act(x_ref[r, span, :]).astype(jnp.bfloat16)
        out_ref[rows + 1, here, :] = (act(below_ref[0, span, :]) * flag_ref[1]).astype(jnp.bfloat16)


def activate(x, around, columns, column):
    n_row = lax.axis_size("row")
    rows, chans, lanes = x.shape
    ci = C // n_row
    count = rows * GROUP_SIZE * WIDTH
    (above, below), stats = around
    r = lax.axis_index("row")
    flags = jnp.stack([r > 0, r < n_row - 1]).astype(jnp.float32)
    vmem = pl.BlockSpec(memory_space=pltpu.VMEM)
    return pl.pallas_call(
        lambda *refs: norm_body(count, n_row, column, *refs),
        in_specs=[pl.BlockSpec(memory_space=pltpu.SMEM)] + [vmem] * (4 + n_row),
        out_shape=[jax.ShapeDtypeStruct((rows + 2, ci, lanes), jnp.bfloat16)] * (chans // ci),
        compiler_params=params(),
        name="norm",
    )(flags, x, above, below, columns, *stats)


def gather_wa(parts):
    n_wa = lax.axis_size("wa")
    pieces = {0: list(parts)}
    bit = n_wa // 2
    while bit:
        for k in sorted(pieces):
            pieces[k | bit] = []
            for part in pieces[k]:
                pieces[k | bit].append(lax.ppermute(part, "wa", xor_pairs(n_wa, bit)))
        bit //= 2
    return [pieces[k] for k in range(n_wa)]


def prepared(kernel, ci, co):
    flat = kernel.reshape(TAPS, TAPS * ci, co)
    turned = jnp.transpose(flat, (2, 0, 1))
    depth = -(-TAPS * ci // 128) * 128
    turned = jnp.pad(turned, ((0, 0), (0, 0), (0, depth - TAPS * ci)))
    return turned.reshape(co, TAPS * depth)


def ring_order(n):
    return list(range(0, n, 2)) + list(range(n - 1, 0, -2))


def ring_blocks():
    n = lax.axis_size("row")
    r = lax.axis_index("row")
    place = jnp.where(r % 2 == 0, r // 2, n - 1 - r // 2)
    shifts = [0]
    for s in range(1, n // 2):
        shifts += [n - s, s]
    shifts.append(n // 2)
    at = (place + jnp.array(shifts, jnp.int32)) % n
    return jnp.where(2 * at < n, 2 * at, 2 * (n - at) - 1)


def ring(own, hold):
    n = lax.axis_size("row")
    order = ring_order(n)
    up = [(order[i], order[(i + 1) % n]) for i in range(n)]
    down = [(d, s) for s, d in up]
    chunks = [own]
    a = b = own
    for s in range(1, n // 2 + 1):
        if s in hold:
            a, b, _ = lax.optimization_barrier((a, b, hold[s]))
        if s == n // 2:
            half = own.shape[0] // 2
            a, b = a[:half], b[half:]
        a = lax.ppermute(a, "row", up)
        b = lax.ppermute(b, "row", down)
        chunks += [a, b]
    return chunks


def conv_body(stage, before, n_chunks, n_wa, idx_ref, chunk_refs, act_refs, acc_ref, wbuf, abuf, xbuf, order, wsem, asem):
    rows, co, lanes = acc_ref.shape
    ci = abuf.shape[2]
    depth = xbuf.shape[2]
    per_shard = n_chunks // n_wa
    me = idx_ref[n_chunks]
    buffers = wbuf.shape[0]

    def piece_of(c):
        return (idx_ref[c] // per_shard) ^ me

    def there(c, at):
        if at is None or c >= at[0]:
            return jnp.bool_(False)
        return piece_of(c) < 2 if at[1] else jnp.bool_(True)

    last = stage[0] == n_chunks
    count = jnp.int32(0)
    for c in range(stage[0]):
        mine = jnp.logical_and(there(c, stage), jnp.logical_not(there(c, before)))

        @pl.when(mine)
        def _():
            order[count] = c

        count += mine.astype(jnp.int32)

    def start(i):
        @pl.when(i < count)
        def _():
            slot = i % buffers
            chunk = order[i]
            act = piece_of(chunk) * per_shard + idx_ref[chunk] % per_shard
            for k in range(len(act_refs)):

                @pl.when(act == k)
                def _():
                    pltpu.make_async_copy(act_refs[k], abuf.at[slot], asem.at[slot]).start()

            for c in range(min(stage[0], n_chunks - 1)):

                @pl.when(chunk == c)
                def _():
                    pltpu.make_async_copy(chunk_refs[c], wbuf.at[slot], wsem.at[slot]).start()

            if last:

                @pl.when(chunk == n_chunks - 1)
                def _():
                    half = co // 2
                    for k in range(2):
                        pltpu.make_async_copy(
                            chunk_refs[n_chunks - 1 + k], wbuf.at[slot, pl.ds(k * half, half), :], wsem.at[slot]
                        ).start()

    def acts_ready(i):
        @pl.when(i < count)
        def _():
            slot = i % buffers
            pltpu.make_async_copy(act_refs[0], abuf.at[slot], asem.at[slot]).wait()

    column = lax.broadcasted_iota(jnp.int32, (ci, lanes), 1) % WIDTH

    def build(i):
        for r in range(rows + 2):
            v = abuf[i % buffers, r]
            zero = jnp.zeros_like(v)
            xbuf[i % 2, r, 0:ci, :] = jnp.where(column == 0, zero, pltpu.roll(v, 1, 1))
            xbuf[i % 2, r, ci : 2 * ci, :] = v
            xbuf[i % 2, r, 2 * ci : 3 * ci, :] = jnp.where(column == WIDTH - 1, zero, pltpu.roll(v, lanes - 1, 1))

    def step(i, carry):
        start(i + 2)
        acts_ready(i + 1)
        pltpu.make_async_copy(chunk_refs[0], wbuf.at[i % buffers], wsem.at[i % buffers]).wait()
        build(i + 1)
        for r in range(rows):
            panel = xbuf[i % 2, r : r + TAPS].reshape(TAPS * depth, lanes)
            acc_ref[r] += jnp.dot(wbuf[i % buffers], panel, preferred_element_type=jnp.float32)
        return carry

    start(jnp.int32(0))
    start(jnp.int32(1))
    if depth > TAPS * ci:
        xbuf[:, :, TAPS * ci :, :] = jnp.zeros((2, rows + 2, depth - TAPS * ci, lanes), jnp.bfloat16)
    acts_ready(jnp.int32(0))
    build(jnp.int32(0))
    lax.fori_loop(0, count, step, 0)


def conv_part(stage, before, idx, chunks, acts, acc, columns, column, summary):
    n_wa = lax.axis_size("wa")
    n_chunks = lax.axis_size("row")
    last = stage[0] == n_chunks
    rows, ci, lanes = acts[0].shape
    rows -= 2
    co, kdim = chunks[0].shape
    depth = kdim // TAPS
    n_in = len(chunks) + len(acts)
    shape = (rows, co, lanes)

    def body(idx_ref, *refs):
        refs = list(refs)
        chunk_refs = refs[: len(chunks)]
        act_refs = refs[len(chunks) : n_in]
        rest = refs[n_in:]
        acc_in = rest.pop(0) if before is not None else None
        columns_ref = rest.pop(0) if last else None
        out_ref = rest.pop(0)
        summary_refs = [rest.pop(0) for _ in range(3)] if summary else None
        acc_ref = rest.pop(0) if last else out_ref
        total_ref = rest.pop(0) if summary else None
        value = jnp.zeros(shape, jnp.float32) if before is None else acc_in[...]
        acc_ref[...] = value + columns_ref[:, column : column + 1][None] if last else value
        conv_body(stage, before, n_chunks, n_wa, idx_ref, chunk_refs, act_refs, acc_ref, *rest)
        if last:
            out_ref[...] = acc_ref[...].astype(jnp.bfloat16)
        if summary:
            summary_refs[0][0] = out_ref[0]
            summary_refs[1][0] = out_ref[rows - 1]
            stats_into(out_ref, summary_refs[2], total_ref)

    any_spec = pl.BlockSpec(memory_space=pl.ANY)
    full = pl.BlockSpec(memory_space=pltpu.VMEM)
    in_specs = [pl.BlockSpec(memory_space=pltpu.SMEM)] + [any_spec] * n_in
    args = [idx] + list(chunks) + list(acts)
    scratch = []
    if before is not None:
        in_specs.append(full)
        args.append(acc)
    if last:
        in_specs.append(full)
        args.append(columns)
        scratch.append(pltpu.VMEM(shape, jnp.float32))
    if summary:
        scratch.append(pltpu.VMEM((co // GROUP_SIZE, lanes), jnp.float32))
    scratch += [
        pltpu.VMEM((3, co, kdim), jnp.bfloat16),
        pltpu.VMEM((3, rows + 2, ci, lanes), jnp.bfloat16),
        pltpu.VMEM((2, rows + 2, depth, lanes), jnp.bfloat16),
        pltpu.SMEM((n_chunks,), jnp.int32),
        pltpu.SemaphoreType.DMA((3,)),
        pltpu.SemaphoreType.DMA((3,)),
    ]
    outs = [jax.ShapeDtypeStruct(shape, jnp.bfloat16 if last else jnp.float32)]
    outs += edge_shapes(shape) if summary else []
    result = pl.pallas_call(
        body,
        in_specs=in_specs,
        out_specs=[full] * len(outs),
        out_shape=outs,
        scratch_shapes=scratch,
        compiler_params=params(),
        name="conv",
    )(*args)
    return result if summary else result[0]


def convolve(parts, chunks, idx, columns, column, summary):
    n = lax.axis_size("row")
    pieces = gather_wa(parts)
    near = pieces[0] + pieces[1]
    every = [p for piece in pieces for p in piece]
    stages = [(n - 3, True), (n - 1, False), (n, False)]
    acc = None
    before = None
    for stage in stages:
        last = stage[0] == n
        acts = near if stage[1] else every
        taken = chunks if last else chunks[: stage[0]]
        acc = conv_part(stage, before, idx, taken, acts, acc, columns, column, summary and last)
        before = stage
    return acc


def per_device(
    activations,
    gain_one,
    shift_one,
    kernel_one,
    bias_one,
    gain_two,
    shift_two,
    kernel_two,
    bias_two,
):
    co = activations.shape[1]
    ci = kernel_one.shape[4] // co
    idx = jnp.concatenate([ring_blocks(), lax.axis_index("wa").astype(jnp.int32)[None]])
    own_one = prepared(kernel_one, ci, co)
    own_two = prepared(kernel_two, ci, co)
    columns = jnp.stack([gain_one, shift_one, bias_one, gain_two, shift_two, bias_two], axis=1)
    idx, own_two, columns = lax.optimization_barrier((idx, own_two, columns))
    around = surroundings(summary_of(activations))
    chunks_one = ring(own_one, {2: (idx, own_two, columns)})
    first = activate(activations, around, columns, 0)
    hidden, *summary = convolve(first, chunks_one, idx, columns, 2, True)
    around = surroundings(summary)
    chunks_two = ring(own_two, {})
    second = activate(hidden, around, columns, 3)
    return convolve(second, chunks_two, idx, columns, 5, False)


def solution(mesh):
    placed = (
        P("row", "wa", None),
        P("wa"),
        P("wa"),
        P(None, None, "row", "wa", None),
        P("wa"),
        P("wa"),
        P("wa"),
        P(None, None, "row", "wa", None),
        P("wa"),
    )

    return jax.shard_map(per_device, mesh=mesh, in_specs=placed, out_specs=P("row", "wa", None), check_vma=False)
```

time: 271 us -> 332 us (1.23)
  waiting for transfers between devices: 111 us -> 176 us
  starting transfers between devices: 69.1 us -> 63.1 us
    ppermute x30, waiting for transfers between devices: 79.8 us -> 142 us  [the longest x14 104 us: surroundings(): every.append(lax.ppermute(stats, 'row', xor_pairs(n_row, k)))]
    ppermute x8, waiting for transfers between devices: 0.04 us -> 17.7 us  [ring(): b = lax.ppermute(b, 'row', down)]
    ppermute x8, waiting for transfers between devices: 31.1 us -> 16.5 us  [ring(): a = lax.ppermute(a, 'row', up)]
    ppermute x30, starting transfers between devices: 51.6 us -> 39.3 us  [the longest x14 24.4 us: surroundings(): every.append(lax.ppermute(stats, 'row', xor_pairs(n_row, k)))]
    broadcast_in_dim x6 -> x0, local copies, waits for them, and re-layouts: 4.64 us -> none  [the longest x2 1.57 us: activate(): shift[:, None]]
    ppermute x8, starting transfers between devices: 5.85 us -> 10.4 us  [ring(): b = lax.ppermute(b, 'row', down)]
    unnamed x76 -> x86, local copies, waits for them, and re-layouts: 2.6 us -> 6.88 us
    pallas_call x8 -> x9, Pallas kernels: 66.3 us -> 69.3 us  [the longest x6 57.4 us: conv_part(): pl.pallas_call(body, in_specs=in_specs, out_specs=[full] * len(outs), out...]
  transfers between devices with their start and end apart: 46 -> 46, of which waited for: 16 -> 23; matrix products, arithmetic and copies ran while one was open for 6% -> 3% of each run, Pallas kernels for 20% -> 19%
where the time goes in v2:
time: 332 us; the launch traced here: 331 us
  waiting for transfers between devices  176 us (53%)
  Pallas kernels  69.3 us (21%)
  starting transfers between devices  63.1 us (19%)
  local copies, waits for them, and re-layouts  20.6 us (6%)
    ppermute x14, waiting for transfers between devices, surroundings(): every.append(lax.ppermute(stats, 'row', xor_pairs(n_row, k)))  104 us
    pallas_call x6, Pallas kernels, conv_part(): pl.pallas_call(body, in_specs=in_specs, out_specs=[full] * len(outs), out...  57.4 us
    ppermute x12, waiting for transfers between devices, gather_wa(): pieces[k | bit].append(lax.ppermute(part, 'wa', xor_pairs(n_wa, bit)))  33.3 us
    ppermute x14, starting transfers between devices, surroundings(): every.append(lax.ppermute(stats, 'row', xor_pairs(n_row, k)))  24.4 us
    ppermute x8, waiting for transfers between devices, ring(): b = lax.ppermute(b, 'row', down)  17.7 us
    ppermute x8, waiting for transfers between devices, ring(): a = lax.ppermute(a, 'row', up)  16.5 us
    ppermute x8, starting transfers between devices, ring(): a = lax.ppermute(a, 'row', up)  13.4 us
    ppermute x8, starting transfers between devices, ring(): b = lax.ppermute(b, 'row', down)  10.4 us
  transfers between devices with their start and end apart: 46, of which 23 were waited for; matrix products, arithmetic and copies ran while one was open for 3% of the time, Pallas kernels for 19%

profile of v2, /device:TPU:0, one launch (start us, length us, event | category | flops | bytes accessed | tf_op | source)
XLA Modules:
  0.0 330.8 jit_solution(15432889159124456043)
XLA Ops:
  0.0 2.9 reshape.14
  3.6 3.1 collective-permute-start.8
  6.7 2.9 reshape.12
  9.7 1.1 pad.7
  11.6 1.5 copy.41.refs_0_
  13.1 2.1 collective-permute-start
  15.2 14.2 %collective-permute-done.8.refs_1_ = bf16[320,1536]{1,0:T(8,128)(2,1)} collective-permute-done((bf16[320,1536]{1,0:T(8,128)(2,1)S(1)}, bf16[320,1536]{1,0:T(8,128)(2,1)}, u32[]{:S(2)}, u32[]{:S(2)}) %collective-permute-start.8) | collective-permute-done | bytes 983072 | tf_op jit(solution)/shard_map/ppermute | solution.py:192
  30.1 1.6 collective-permute-start.10
  32.1 3.2 stats.1
  35.3 3.2 collective-permute-start.16
  38.6 1.8 collective-permute-start.18
  40.3 30.4 %collective-permute-done.18.refs_6_ = f32[2,8,128]{2,1,0:T(8,128)S(1)} collective-permute-done((f32[2,8,128]{2,1,0:T(8,128)}, f32[2,8,128]{2,1,0:T(8,128)S(1)}, u32[]{:S(2)}, u32[]{:S(2)}) %collective-permute-start.18) | collective-permute-done | bytes 8224 | tf_op jit(solution)/shard_map/ppermute | solution.py:88
  70.7 3.9 %collective-permute-done.19.refs_7_ = f32[2,8,128]{2,1,0:T(8,128)S(1)} collective-permute-done((f32[2,8,128]{2,1,0:T(8,128)}, f32[2,8,128]{2,1,0:T(8,128)S(1)}, u32[]{:S(2)}, u32[]{:S(2)}) %collective-permute-start.19) | collective-permute-done | bytes 8224 | tf_op jit(solution)/shard_map/ppermute | solution.py:88
  74.6 4.8 %collective-permute-done.20.refs_8_ = f32[2,8,128]{2,1,0:T(8,128)S(1)} collective-permute-done((f32[2,8,128]{2,1,0:T(8,128)}, f32[2,8,128]{2,1,0:T(8,128)S(1)}, u32[]{:S(2)}, u32[]{:S(2)}) %collective-permute-start.20) | collective-permute-done | bytes 8224 | tf_op jit(solution)/shard_map/ppermute | solution.py:88
  79.4 9.4 %collective-permute-start.21 = (f32[2,8,128]{2,1,0:T(8,128)}, f32[2,8,128]{2,1,0:T(8,128)S(1)}, u32[]{:S(2)}, u32[]{:S(2)}) collective-permute-start(f32[2,8,128]{2,1,0:T(8,128)} %get-tuple-element.28.refs_5_), channel_id=1, source_target_pairs={{0,4},{1,5},{2,6},{3,7},{4,0},{5,1},{6,2},{7,3},{8,12},{9,13},{10,... | collective-permute-start | bytes 24584 | tf_op jit(solution)/shard_map/ppermute | solution.py:88
  88.8 1.8 collective-permute-done.21.refs_9_
  90.6 3.8 %collective-permute-start.22 = (f32[2,8,128]{2,1,0:T(8,128)}, f32[2,8,128]{2,1,0:T(8,128)S(1)}, u32[]{:S(2)}, u32[]{:S(2)}) collective-permute-start(f32[2,8,128]{2,1,0:T(8,128)} %get-tuple-element.28.refs_5_), channel_id=1, source_target_pairs={{0,5},{1,4},{2,7},{3,6},{4,1},{5,0},{6,3},{7,2},{8,13},{9,12},{10,... | collective-permute-start | bytes 24584 | tf_op jit(solution)/shard_map/ppermute | solution.py:88
  94.4 1.8 collective-permute-done.22.refs_10_
  96.3 3.4 %collective-permute-start.23 = (f32[2,8,128]{2,1,0:T(8,128)}, f32[2,8,128]{2,1,0:T(8,128)S(1)}, u32[]{:S(2)}, u32[]{:S(2)}) collective-permute-start(f32[2,8,128]{2,1,0:T(8,128)} %get-tuple-element.28.refs_5_), channel_id=1, source_target_pairs={{0,6},{1,7},{2,4},{3,5},{4,2},{5,3},{6,0},{7,1},{8,14},{9,15},{10,... | collective-permute-start | bytes 24584 | tf_op jit(solution)/shard_map/ppermute | solution.py:88
  99.7 2.3 collective-permute-done.23.refs_11_
  102.0 5.3 %collective-permute-start.24 = (f32[2,8,128]{2,1,0:T(8,128)}, f32[2,8,128]{2,1,0:T(8,128)S(1)}, u32[]{:S(2)}, u32[]{:S(2)}) collective-permute-start(f32[2,8,128]{2,1,0:T(8,128)} %get-tuple-element.28.refs_5_), channel_id=1, source_target_pairs={{0,7},{1,6},{2,5},{3,4},{4,3},{5,2},{6,1},{7,0},{8,15},{9,14},{10,... | collective-permute-start | bytes 24584 | tf_op jit(solution)/shard_map/ppermute | solution.py:88
  107.3 1.9 collective-permute-done.24.refs_12_
  109.3 1.3 collective-permute-start.17
  110.6 2.7 collective-permute-start.1
  113.3 0.8 copy.33.refs_4_.refs_18_
  114.8 3.8 %collective-permute-done.17.refs_3_ = bf16[1,320,512]{2,1,0:T(8,128)(2,1)} collective-permute-done((bf16[1,320,512]{2,1,0:T(8,128)(2,1)}, bf16[1,320,512]{2,1,0:T(8,128)(2,1)}, u32[]{:S(2)}, u32[]{:S(2)}) %collective-permute-start.17) | collective-permute-done | bytes 327712 | tf_op jit(solution)/shard_map/ppermute | solution.py:85
  118.6 4.3 %norm.2 = (bf16[5,160,512]{2,1,0:T(8,128)(2,1)}, bf16[5,160,512]{2,1,0:T(8,128)(2,1)}) custom-call(f32[2]{0:T(128)} %add_convert_fusion.refs_0_, bf16[3,320,512]{2,1,0:T(8,128)(2,1)} %refs_1_.1, bf16[1,320,512]{2,1,0:T(8,128)(2,1)} %copy-done.19, bf16[1,320,512]{2,1,0:T(8,128)(2,1)} %collective-permute-done.17.refs_3_, f32[320,6]{1,0:T(8,128)} %copy.33.refs_4_.refs_18_, ...), custom_call_target="tpu_custom_call" | custom-call | tf_op jit(solution)/shard_map/norm/pallas_call | solution.py:133
  122.9 1.5 collective-permute-start.27
  125.0 3.9 %collective-permute-start.12 = (bf16[320,1536]{1,0:T(8,128)(2,1)}, bf16[320,1536]{1,0:T(8,128)(2,1)S(1)}, u32[]{:S(2)}, u32[]{:S(2)}) collective-permute-start(bf16[320,1536]{1,0:T(8,128)(2,1)} %collective-permute-done.10.refs_3_), channel_id=1, source_target_pairs={{0,2},{2,4},{4,6},{6,7},{7,5},{5,3},{3,1},{1,0},{8,10},{10,12},{12... | collective-permute-start | bytes 2949128 | tf_op jit(solution)/shard_map/ppermute | solution.py:192
  128.9 2.0 collective-permute-start.13
  130.8 13.0 %collective-permute-done.1.refs_2_ = bf16[320,1536]{1,0:T(8,128)(2,1)S(1)} collective-permute-done((bf16[320,1536]{1,0:T(8,128)(2,1)S(1)}, bf16[320,1536]{1,0:T(8,128)(2,1)S(1)}, u32[]{:S(2)}, u32[]{:S(2)}) %collective-permute-start.1) | collective-permute-done | bytes 983072 | tf_op jit(solution)/shard_map/ppermute | solution.py:193
  144.4 7.7 %collective-permute-done.28.refs_12_.refs_14_ = bf16[5,160,512]{2,1,0:T(8,128)(2,1)} collective-permute-done((bf16[5,160,512]{2,1,0:T(8,128)(2,1)}, bf16[5,160,512]{2,1,0:T(8,128)(2,1)}, u32[]{:S(2)}, u32[]{:S(2)}) %collective-permute-start.28) | collective-permute-done | bytes 819232 | tf_op jit(solution)/shard_map/ppermute | solution.py:150
  152.6 4.0 %collective-permute-done.13.refs_6_ = bf16[320,1536]{1,0:T(8,128)(2,1)S(1)} collective-permute-done((bf16[320,1536]{1,0:T(8,128)(2,1)}, bf16[320,1536]{1,0:T(8,128)(2,1)S(1)}, u32[]{:S(2)}, u32[]{:S(2)}) %collective-permute-start.13) | collective-permute-done | bytes 983072 | tf_op jit(solution)/shard_map/ppermute | solution.py:193
  156.7 0.9 slice.18
  157.6 0.8 slice.19
  159.0 1.4 collective-permute-start.15
  160.5 0.9 copy-done.13
  161.4 2.0 collective-permute-start.3
  163.3 11.9 %conv.6.refs_15_ = f32[3,320,512]{2,1,0:T(8,128)} custom-call(s32[9]{0:T(128)} %pad_add_fusion.idx_ref, bf16[320,1536]{1,0:T(8,128)(2,1)} %copy-done.1, bf16[320,1536]{1,0:T(8,128)(2,1)} %collective-permute-done.8.refs_1_, bf16[320,1536]{1,0:T(8,128)(2,1)} %collective-permute-done.9.refs_2_, bf16[320,1536]{1,0:T(8,128)(2,1)} %collective-permute-done.10.refs_3_, ...), custom_call_target="tpu_custom_call" | custom-call | tf_op jit(solution)/shard_map/conv/pallas_call | solution.py:344
  175.2 10.3 %conv.7.refs_17_ = f32[3,320,512]{2,1,0:T(8,128)} custom-call(s32[9]{0:T(128)} %pad_add_fusion.idx_ref, bf16[320,1536]{1,0:T(8,128)(2,1)} %copy-done.1, bf16[320,1536]{1,0:T(8,128)(2,1)} %collective-permute-done.8.refs_1_, bf16[320,1536]{1,0:T(8,128)(2,1)} %collective-permute-done.9.refs_2_, bf16[320,1536]{1,0:T(8,128)(2,1)} %collective-permute-done.10.refs_3_, ...), custom_call_target="tpu_custom_call" | custom-call | tf_op jit(solution)/shard_map/conv/pallas_call | solution.py:344
  185.6 2.3 collective-permute-done.14.refs_7_
  189.5 6.8 %conv.8 = (bf16[3,320,512]{2,1,0:T(8,128)(2,1)}, bf16[1,320,512]{2,1,0:T(8,128)(2,1)}, bf16[1,320,512]{2,1,0:T(8,128)(2,1)}, f32[2,8,128]{2,1,0:T(8,128)}) custom-call(s32[9]{0:T(128)} %pad_add_fusion.idx_ref, bf16[320,1536]{1,0:T(8,128)(2,1)} %copy-done.1, bf16[320,1536]{1,0:T(8,128)(2,1)} %collective-permute-done.8.refs_1_, ...), custom_call_target="tpu_custom_call" | custom-call | tf_op jit(solution)/shard_map/conv/pallas_call | solution.py:344
  196.3 3.5 %collective-permute-start.31 = (bf16[1,320,512]{2,1,0:T(8,128)(2,1)}, bf16[1,320,512]{2,1,0:T(8,128)(2,1)S(1)}, u32[]{:S(2)}, u32[]{:S(2)}) collective-permute-start(bf16[1,320,512]{2,1,0:T(8,128)(2,1)} %get-tuple-element.32), channel_id=1, source_target_pairs={{0,1},{1,2},{2,3},{3,4},{4,5},{5,6},{6,7},{8,9},{9,10},{10,11},{11... | collective-permute-start | bytes 983048 | tf_op jit(solution)/shard_map/ppermute | solution.py:84
  199.8 1.3 collective-permute-start.32
  201.2 2.1 collective-permute-start.4
  203.9 26.2 %collective-permute-done.33.refs_6_ = f32[2,8,128]{2,1,0:T(8,128)S(1)} collective-permute-done((f32[2,8,128]{2,1,0:T(8,128)}, f32[2,8,128]{2,1,0:T(8,128)S(1)}, u32[]{:S(2)}, u32[]{:S(2)}) %collective-permute-start.33) | collective-permute-done | bytes 8224 | tf_op jit(solution)/shard_map/ppermute | solution.py:88
  230.2 3.9 %collective-permute-done.34.refs_7_ = f32[2,8,128]{2,1,0:T(8,128)S(1)} collective-permute-done((f32[2,8,128]{2,1,0:T(8,128)}, f32[2,8,128]{2,1,0:T(8,128)S(1)}, u32[]{:S(2)}, u32[]{:S(2)}) %collective-permute-start.34) | collective-permute-done | bytes 8224 | tf_op jit(solution)/shard_map/ppermute | solution.py:88
  234.0 4.8 %collective-permute-done.35.refs_8_ = f32[2,8,128]{2,1,0:T(8,128)S(1)} collective-permute-done((f32[2,8,128]{2,1,0:T(8,128)}, f32[2,8,128]{2,1,0:T(8,128)S(1)}, u32[]{:S(2)}, u32[]{:S(2)}) %collective-permute-start.35) | collective-permute-done | bytes 8224 | tf_op jit(solution)/shard_map/ppermute | solution.py:88
  238.8 4.8 %collective-permute-done.36.refs_9_ = f32[2,8,128]{2,1,0:T(8,128)S(1)} collective-permute-done((f32[2,8,128]{2,1,0:T(8,128)}, f32[2,8,128]{2,1,0:T(8,128)S(1)}, u32[]{:S(2)}, u32[]{:S(2)}) %collective-permute-start.36) | collective-permute-done | bytes 8224 | tf_op jit(solution)/shard_map/ppermute | solution.py:88
  243.6 5.7 %collective-permute-done.37.refs_10_ = f32[2,8,128]{2,1,0:T(8,128)S(1)} collective-permute-done((f32[2,8,128]{2,1,0:T(8,128)}, f32[2,8,128]{2,1,0:T(8,128)S(1)}, u32[]{:S(2)}, u32[]{:S(2)}) %collective-permute-start.37) | collective-permute-done | bytes 8224 | tf_op jit(solution)/shard_map/ppermute | solution.py:88
  249.2 5.7 %collective-permute-done.38.refs_11_ = f32[2,8,128]{2,1,0:T(8,128)S(1)} collective-permute-done((f32[2,8,128]{2,1,0:T(8,128)}, f32[2,8,128]{2,1,0:T(8,128)S(1)}, u32[]{:S(2)}, u32[]{:S(2)}) %collective-permute-start.38) | collective-permute-done | bytes 8224 | tf_op jit(solution)/shard_map/ppermute | solution.py:88
  254.9 6.6 %collective-permute-done.39.refs_12_ = f32[2,8,128]{2,1,0:T(8,128)S(1)} collective-permute-done((f32[2,8,128]{2,1,0:T(8,128)}, f32[2,8,128]{2,1,0:T(8,128)S(1)}, u32[]{:S(2)}, u32[]{:S(2)}) %collective-permute-start.39) | collective-permute-done | bytes 8224 | tf_op jit(solution)/shard_map/ppermute | solution.py:88
  262.3 4.4 %norm.3 = (bf16[5,160,512]{2,1,0:T(8,128)(2,1)}, bf16[5,160,512]{2,1,0:T(8,128)(2,1)}) custom-call(f32[2]{0:T(128)} %add_convert_fusion.refs_0_, bf16[3,320,512]{2,1,0:T(8,128)(2,1)} %get-tuple-element.31.refs_1_, bf16[1,320,512]{2,1,0:T(8,128)(2,1)} %copy-done.20, bf16[1,320,512]{2,1,0:T(8,128)(2,1)} %copy-done.21, f32[320,6]{1,0:T(8,128)} %copy.33.refs_4_.refs_18_, ...), custom_call_target="tpu_custom_call" | custom-call | tf_op jit(solution)/shard_map/norm/pallas_call | solution.py:133
  266.7 1.5 collective-permute-start.42
  269.3 16.8 %collective-permute-done.42.refs_11_.refs_13_ = bf16[5,160,512]{2,1,0:T(8,128)(2,1)} collective-permute-done((bf16[5,160,512]{2,1,0:T(8,128)(2,1)}, bf16[5,160,512]{2,1,0:T(8,128)(2,1)}, u32[]{:S(2)}, u32[]{:S(2)}) %collective-permute-start.42) | collective-permute-done | bytes 819232 | tf_op jit(solution)/shard_map/ppermute | solution.py:150
  286.0 8.8 %collective-permute-done.43.refs_12_.refs_14_ = bf16[5,160,512]{2,1,0:T(8,128)(2,1)} collective-permute-done((bf16[5,160,512]{2,1,0:T(8,128)(2,1)}, bf16[5,160,512]{2,1,0:T(8,128)(2,1)}, u32[]{:S(2)}, u32[]{:S(2)}) %collective-permute-start.43) | collective-permute-done | bytes 819232 | tf_op jit(solution)/shard_map/ppermute | solution.py:150
  294.8 1.1 slice.16
  296.0 0.9 slice.17
  297.0 1.8 collective-permute-start.7
  298.9 0.9 copy-done.8
  299.8 11.9 %conv.9.refs_15_ = f32[3,320,512]{2,1,0:T(8,128)} custom-call(s32[9]{0:T(128)} %pad_add_fusion.idx_ref, bf16[320,1536]{1,0:T(8,128)(2,1)} %copy-done, bf16[320,1536]{1,0:T(8,128)(2,1)} %copy-done.2, bf16[320,1536]{1,0:T(8,128)(2,1)} %copy-done.3, bf16[320,1536]{1,0:T(8,128)(2,1)} %copy-done.4, bf16[320,1536]{1,0:T(8,128)(2,1)} %collective-permute-done.3.refs_4_, ...), custom_call_target="tpu_custom_call" | custom-call | tf_op jit(solution)/shard_map/conv/pallas_call | solution.py:344
  311.7 0.9 copy-done.14
  312.6 10.3 %conv.10.refs_17_ = f32[3,320,512]{2,1,0:T(8,128)} custom-call(s32[9]{0:T(128)} %pad_add_fusion.idx_ref, bf16[320,1536]{1,0:T(8,128)(2,1)} %copy-done, bf16[320,1536]{1,0:T(8,128)(2,1)} %copy-done.2, bf16[320,1536]{1,0:T(8,128)(2,1)} %copy-done.3, bf16[320,1536]{1,0:T(8,128)(2,1)} %copy-done.4, bf16[320,1536]{1,0:T(8,128)(2,1)} %collective-permute-done.3.refs_4_, ...), custom_call_target="tpu_custom_call" | custom-call | tf_op jit(solution)/shard_map/conv/pallas_call | solution.py:344
  324.6 6.0 %conv.11 = bf16[3,320,512]{2,1,0:T(8,128)(2,1)} custom-call(s32[9]{0:T(128)} %pad_add_fusion.idx_ref, bf16[320,1536]{1,0:T(8,128)(2,1)} %copy-done, bf16[320,1536]{1,0:T(8,128)(2,1)} %copy-done.2, bf16[320,1536]{1,0:T(8,128)(2,1)} %copy-done.3, bf16[320,1536]{1,0:T(8,128)(2,1)} %copy-done.4, bf16[320,1536]{1,0:T(8,128)(2,1)} %collective-permute-done.3.refs_4_, ...), custom_call_target="tpu_custom_call" | custom-call | tf_op jit(solution)/shard_map/conv/pallas_call | solution.py:344
  (144 shorter events, 11.3 us)
Async XLA Ops:
  3.6 25.7 %collective-permute-start.8 = (bf16[320,1536]{1,0:T(8,128)(2,1)S(1)}, bf16[320,1536]{1,0:T(8,128)(2,1)}, u32[]{:S(2)}, u32[]{:S(2)}) collective-permute-start(bf16[320,1536]{1,0:T(8,128)(2,1)S(1)} %copy.36.refs_0_), channel_id=1, source_target_pairs={{0,2},{2,4},{4,6},{6,7},{7,5},{5,3},{3,1},{1,0},{8,10},{10,12},{12... | collective-permute-start | bytes 2949128 | tf_op jit(solution)/shard_map/ppermute | solution.py:192
  6.7 23.3 %collective-permute-start.9 = (bf16[320,1536]{1,0:T(8,128)(2,1)S(1)}, bf16[320,1536]{1,0:T(8,128)(2,1)}, u32[]{:S(2)}, u32[]{:S(2)}) collective-permute-start(bf16[320,1536]{1,0:T(8,128)(2,1)S(1)} %copy.36.refs_0_), channel_id=1, source_target_pairs={{2,0},{4,2},{6,4},{7,6},{5,7},{3,5},{1,3},{0,1},{10,8},{12,10},{14... | collective-permute-start | bytes 2949128 | tf_op jit(solution)/shard_map/ppermute | solution.py:193
  13.1 109.8 %copy-start = (bf16[320,1536]{1,0:T(8,128)(2,1)}, bf16[320,1536]{1,0:T(8,128)(2,1)S(1)}, u32[]{:S(2)}) copy-start(bf16[320,1536]{1,0:T(8,128)(2,1)S(1)} %copy.41.refs_0_) | copy-start | bytes 2949124
  13.1 111.4 %collective-permute-start = (bf16[320,1536]{1,0:T(8,128)(2,1)S(1)}, bf16[320,1536]{1,0:T(8,128)(2,1)S(1)}, u32[]{:S(2)}, u32[]{:S(2)}) collective-permute-start(bf16[320,1536]{1,0:T(8,128)(2,1)S(1)} %copy.41.refs_0_), channel_id=1, source_target_pairs={{0,2},{2,4},{4,6},{6,7},{7,5},{5,3},{3,1},{1,0},{8,10},{10,12},{12... | collective-permute-start | bytes 2949128 | tf_op jit(solution)/shard_map/ppermute | solution.py:192
  30.1 94.9 %collective-permute-start.10 = (bf16[320,1536]{1,0:T(8,128)(2,1)}, bf16[320,1536]{1,0:T(8,128)(2,1)}, u32[]{:S(2)}, u32[]{:S(2)}) collective-permute-start(bf16[320,1536]{1,0:T(8,128)(2,1)} %collective-permute-done.8.refs_1_), channel_id=1, source_target_pairs={{0,2},{2,4},{4,6},{6,7},{7,5},{5,3},{3,1},{1,0},{8,10},{10,12},{12... | collective-permute-start | bytes 2949128 | tf_op jit(solution)/shard_map/ppermute | solution.py:192
  31.6 97.2 %collective-permute-start.11 = (bf16[320,1536]{1,0:T(8,128)(2,1)}, bf16[320,1536]{1,0:T(8,128)(2,1)}, u32[]{:S(2)}, u32[]{:S(2)}) collective-permute-start(bf16[320,1536]{1,0:T(8,128)(2,1)} %collective-permute-done.9.refs_2_), channel_id=1, source_target_pairs={{2,0},{4,2},{6,4},{7,6},{5,7},{3,5},{1,3},{0,1},{10,8},{12,10},{14... | collective-permute-start | bytes 2949128 | tf_op jit(solution)/shard_map/ppermute | solution.py:193
  35.3 75.2 %collective-permute-start.16 = (bf16[1,320,512]{2,1,0:T(8,128)(2,1)}, bf16[1,320,512]{2,1,0:T(8,128)(2,1)S(1)}, u32[]{:S(2)}, u32[]{:S(2)}) collective-permute-start(bf16[1,320,512]{2,1,0:T(8,128)(2,1)} %get-tuple-element.26), channel_id=1, source_target_pairs={{0,1},{1,2},{2,3},{3,4},{4,5},{5,6},{6,7},{8,9},{9,10},{10,11},{11... | collective-permute-start | bytes 983048 | tf_op jit(solution)/shard_map/ppermute | solution.py:84
  38.6 32.2 %collective-permute-start.18 = (f32[2,8,128]{2,1,0:T(8,128)}, f32[2,8,128]{2,1,0:T(8,128)S(1)}, u32[]{:S(2)}, u32[]{:S(2)}) collective-permute-start(f32[2,8,128]{2,1,0:T(8,128)} %get-tuple-element.28.refs_5_), channel_id=1, source_target_pairs={{0,1},{1,0},{2,3},{3,2},{4,5},{5,4},{6,7},{7,6},{8,9},{9,8},{10,11... | collective-permute-start | bytes 24584 | tf_op jit(solution)/shard_map/ppermute | solution.py:88
  70.7 47.8 %copy-start.22 = (f32[2,8,128]{2,1,0:T(8,128)}, f32[2,8,128]{2,1,0:T(8,128)S(1)}, u32[]{:S(2)}) copy-start(f32[2,8,128]{2,1,0:T(8,128)S(1)} %collective-permute-done.18.refs_6_) | copy-start | bytes 24580
  70.7 3.9 %collective-permute-start.19 = (f32[2,8,128]{2,1,0:T(8,128)}, f32[2,8,128]{2,1,0:T(8,128)S(1)}, u32[]{:S(2)}, u32[]{:S(2)}) collective-permute-start(f32[2,8,128]{2,1,0:T(8,128)} %get-tuple-element.28.refs_5_), channel_id=1, source_target_pairs={{0,2},{1,3},{2,0},{3,1},{4,6},{5,7},{6,4},{7,5},{8,10},{9,11},{10,... | collective-permute-start | bytes 24584 | tf_op jit(solution)/shard_map/ppermute | solution.py:88
  74.6 44.0 %copy-start.23 = (f32[2,8,128]{2,1,0:T(8,128)}, f32[2,8,128]{2,1,0:T(8,128)S(1)}, u32[]{:S(2)}) copy-start(f32[2,8,128]{2,1,0:T(8,128)S(1)} %collective-permute-done.19.refs_7_) | copy-start | bytes 24580
  74.6 4.8 %collective-permute-start.20 = (f32[2,8,128]{2,1,0:T(8,128)}, f32[2,8,128]{2,1,0:T(8,128)S(1)}, u32[]{:S(2)}, u32[]{:S(2)}) collective-permute-start(f32[2,8,128]{2,1,0:T(8,128)} %get-tuple-element.28.refs_5_), channel_id=1, source_target_pairs={{0,3},{1,2},{2,1},{3,0},{4,7},{5,6},{6,5},{7,4},{8,11},{9,10},{10,... | collective-permute-start | bytes 24584 | tf_op jit(solution)/shard_map/ppermute | solution.py:88
  79.4 39.2 %copy-start.24 = (f32[2,8,128]{2,1,0:T(8,128)}, f32[2,8,128]{2,1,0:T(8,128)S(1)}, u32[]{:S(2)}) copy-start(f32[2,8,128]{2,1,0:T(8,128)S(1)} %collective-permute-done.20.refs_8_) | copy-start | bytes 24580
  79.4 11.3 %collective-permute-start.21 = (f32[2,8,128]{2,1,0:T(8,128)}, f32[2,8,128]{2,1,0:T(8,128)S(1)}, u32[]{:S(2)}, u32[]{:S(2)}) collective-permute-start(f32[2,8,128]{2,1,0:T(8,128)} %get-tuple-element.28.refs_5_), channel_id=1, source_target_pairs={{0,4},{1,5},{2,6},{3,7},{4,0},{5,1},{6,2},{7,3},{8,12},{9,13},{10,... | collective-permute-start | bytes 24584 | tf_op jit(solution)/shard_map/ppermute | solution.py:88
  90.6 27.9 %copy-start.26 = (f32[2,8,128]{2,1,0:T(8,128)}, f32[2,8,128]{2,1,0:T(8,128)S(1)}, u32[]{:S(2)}) copy-start(f32[2,8,128]{2,1,0:T(8,128)S(1)} %collective-permute-done.21.refs_9_) | copy-start | bytes 24580
  90.6 5.7 %collective-permute-start.22 = (f32[2,8,128]{2,1,0:T(8,128)}, f32[2,8,128]{2,1,0:T(8,128)S(1)}, u32[]{:S(2)}, u32[]{:S(2)}) collective-permute-start(f32[2,8,128]{2,1,0:T(8,128)} %get-tuple-element.28.refs_5_), channel_id=1, source_target_pairs={{0,5},{1,4},{2,7},{3,6},{4,1},{5,0},{6,3},{7,2},{8,13},{9,12},{10,... | collective-permute-start | bytes 24584 | tf_op jit(solution)/shard_map/ppermute | solution.py:88
  96.3 22.3 %copy-start.28 = (f32[2,8,128]{2,1,0:T(8,128)}, f32[2,8,128]{2,1,0:T(8,128)S(1)}, u32[]{:S(2)}) copy-start(f32[2,8,128]{2,1,0:T(8,128)S(1)} %collective-permute-done.22.refs_10_) | copy-start | bytes 24580
  96.3 5.7 %collective-permute-start.23 = (f32[2,8,128]{2,1,0:T(8,128)}, f32[2,8,128]{2,1,0:T(8,128)S(1)}, u32[]{:S(2)}, u32[]{:S(2)}) collective-permute-start(f32[2,8,128]{2,1,0:T(8,128)} %get-tuple-element.28.refs_5_), channel_id=1, source_target_pairs={{0,6},{1,7},{2,4},{3,5},{4,2},{5,3},{6,0},{7,1},{8,14},{9,15},{10,... | collective-permute-start | bytes 24584 | tf_op jit(solution)/shard_map/ppermute | solution.py:88
  102.0 16.6 %copy-start.30 = (f32[2,8,128]{2,1,0:T(8,128)}, f32[2,8,128]{2,1,0:T(8,128)S(1)}, u32[]{:S(2)}) copy-start(f32[2,8,128]{2,1,0:T(8,128)S(1)} %collective-permute-done.23.refs_11_) | copy-start | bytes 24580
  102.0 7.3 %collective-permute-start.24 = (f32[2,8,128]{2,1,0:T(8,128)}, f32[2,8,128]{2,1,0:T(8,128)S(1)}, u32[]{:S(2)}, u32[]{:S(2)}) collective-permute-start(f32[2,8,128]{2,1,0:T(8,128)} %get-tuple-element.28.refs_5_), channel_id=1, source_target_pairs={{0,7},{1,6},{2,5},{3,4},{4,3},{5,2},{6,1},{7,0},{8,15},{9,14},{10,... | collective-permute-start | bytes 24584 | tf_op jit(solution)/shard_map/ppermute | solution.py:88
  109.3 9.3 %copy-start.32 = (f32[2,8,128]{2,1,0:T(8,128)}, f32[2,8,128]{2,1,0:T(8,128)S(1)}, u32[]{:S(2)}) copy-start(f32[2,8,128]{2,1,0:T(8,128)S(1)} %collective-permute-done.24.refs_12_) | copy-start | bytes 24580
  109.3 9.3 %collective-permute-start.17 = (bf16[1,320,512]{2,1,0:T(8,128)(2,1)}, bf16[1,320,512]{2,1,0:T(8,128)(2,1)}, u32[]{:S(2)}, u32[]{:S(2)}) collective-permute-start(bf16[1,320,512]{2,1,0:T(8,128)(2,1)} %get-tuple-element.27), channel_id=1, source_target_pairs={{1,0},{2,1},{3,2},{4,3},{5,4},{6,5},{7,6},{9,8},{10,9},{11,10},{12... | collective-permute-start | bytes 983048 | tf_op jit(solution)/shard_map/ppermute | solution.py:85
  110.6 33.3 %collective-permute-start.1 = (bf16[320,1536]{1,0:T(8,128)(2,1)S(1)}, bf16[320,1536]{1,0:T(8,128)(2,1)S(1)}, u32[]{:S(2)}, u32[]{:S(2)}) collective-permute-start(bf16[320,1536]{1,0:T(8,128)(2,1)S(1)} %copy.41.refs_0_), channel_id=1, source_target_pairs={{2,0},{4,2},{6,4},{7,6},{5,7},{3,5},{1,3},{0,1},{10,8},{12,10},{14... | collective-permute-start | bytes 2949128 | tf_op jit(solution)/shard_map/ppermute | solution.py:193
  122.9 20.9 %collective-permute-start.27 = (bf16[5,160,512]{2,1,0:T(8,128)(2,1)}, bf16[5,160,512]{2,1,0:T(8,128)(2,1)S(1)}, u32[]{:S(2)}, u32[]{:S(2)}) collective-permute-start(bf16[5,160,512]{2,1,0:T(8,128)(2,1)} %get-tuple-element.29.refs_5_.refs_7_.refs_9_), channel_id=1, source_target_pairs={{0,16},{8,24},{16,0},{24,8},{1,17},{9,25},{17,1},{25,9},{2,18},{10... | collective-permute-start | bytes 2457608 | tf_op jit(solution)/shard_map/ppermute | solution.py:150
  124.5 50.8 %copy-start.2 = (bf16[320,1536]{1,0:T(8,128)(2,1)}, bf16[320,1536]{1,0:T(8,128)(2,1)S(1)}, u32[]{:S(2)}) copy-start(bf16[320,1536]{1,0:T(8,128)(2,1)S(1)} %collective-permute-done.refs_1_) | copy-start | bytes 2949124
  124.5 27.7 %collective-permute-start.28 = (bf16[5,160,512]{2,1,0:T(8,128)(2,1)}, bf16[5,160,512]{2,1,0:T(8,128)(2,1)}, u32[]{:S(2)}, u32[]{:S(2)}) collective-permute-start(bf16[5,160,512]{2,1,0:T(8,128)(2,1)} %get-tuple-element.30.refs_6_.refs_8_.refs_10_), channel_id=1, source_target_pairs={{0,16},{8,24},{16,0},{24,8},{1,17},{9,25},{17,1},{25,9},{2,18},{10... | collective-permute-start | bytes 2457608 | tf_op jit(solution)/shard_map/ppermute | solution.py:150
  125.0 27.2 %collective-permute-start.12 = (bf16[320,1536]{1,0:T(8,128)(2,1)}, bf16[320,1536]{1,0:T(8,128)(2,1)S(1)}, u32[]{:S(2)}, u32[]{:S(2)}) collective-permute-start(bf16[320,1536]{1,0:T(8,128)(2,1)} %collective-permute-done.10.refs_3_), channel_id=1, source_target_pairs={{0,2},{2,4},{4,6},{6,7},{7,5},{5,3},{3,1},{1,0},{8,10},{10,12},{12... | collective-permute-start | bytes 2949128 | tf_op jit(solution)/shard_map/ppermute | solution.py:192
  128.9 27.8 %collective-permute-start.13 = (bf16[320,1536]{1,0:T(8,128)(2,1)}, bf16[320,1536]{1,0:T(8,128)(2,1)S(1)}, u32[]{:S(2)}, u32[]{:S(2)}) collective-permute-start(bf16[320,1536]{1,0:T(8,128)(2,1)} %collective-permute-done.11.refs_4_), channel_id=1, source_target_pairs={{2,0},{4,2},{6,4},{7,6},{5,7},{3,5},{1,3},{0,1},{10,8},{12,10},{14... | collective-permute-start | bytes 2949128 | tf_op jit(solution)/shard_map/ppermute | solution.py:193
  143.9 31.4 %copy-start.3 = (bf16[320,1536]{1,0:T(8,128)(2,1)}, bf16[320,1536]{1,0:T(8,128)(2,1)S(1)}, u32[]{:S(2)}) copy-start(bf16[320,1536]{1,0:T(8,128)(2,1)S(1)} %collective-permute-done.1.refs_2_) | copy-start | bytes 2949124
  143.9 14.5 %collective-permute-start.25 = (bf16[5,160,512]{2,1,0:T(8,128)(2,1)}, bf16[5,160,512]{2,1,0:T(8,128)(2,1)S(1)}, u32[]{:S(2)}, u32[]{:S(2)}) collective-permute-start(bf16[5,160,512]{2,1,0:T(8,128)(2,1)} %get-tuple-element.29.refs_5_.refs_7_.refs_9_), channel_id=1, source_target_pairs={{0,8},{8,0},{16,24},{24,16},{1,9},{9,1},{17,25},{25,17},{2,10},{10... | collective-permute-start | bytes 2457608 | tf_op jit(solution)/shard_map/ppermute | solution.py:150
  143.9 16.6 %copy-start.12 = (bf16[5,160,512]{2,1,0:T(8,128)(2,1)}, bf16[5,160,512]{2,1,0:T(8,128)(2,1)S(1)}, u32[]{:S(2)}) copy-start(bf16[5,160,512]{2,1,0:T(8,128)(2,1)S(1)} %collective-permute-done.27.refs_11_.refs_13_) | copy-start | bytes 2457604
  143.9 15.1 %collective-permute-start.26 = (bf16[5,160,512]{2,1,0:T(8,128)(2,1)}, bf16[5,160,512]{2,1,0:T(8,128)(2,1)S(1)}, u32[]{:S(2)}, u32[]{:S(2)}) collective-permute-start(bf16[5,160,512]{2,1,0:T(8,128)(2,1)} %get-tuple-element.30.refs_6_.refs_8_.refs_10_), channel_id=1, source_target_pairs={{0,8},{8,0},{16,24},{24,16},{1,9},{9,1},{17,25},{25,17},{2,10},{10... | collective-permute-start | bytes 2457608 | tf_op jit(solution)/shard_map/ppermute | solution.py:150
  152.1 8.3 %collective-permute-start.29 = (bf16[5,160,512]{2,1,0:T(8,128)(2,1)S(1)}, bf16[5,160,512]{2,1,0:T(8,128)(2,1)S(1)}, u32[]{:S(2)}, u32[]{:S(2)}) collective-permute-start(bf16[5,160,512]{2,1,0:T(8,128)(2,1)S(1)} %collective-permute-done.27.refs_11_.refs_13_), channel_id=1, source_target_pairs={{0,8},{8,0},{16,24},{24,16},{1,9},{9,1},{17,25},{25,17},{2,10},{10... | collective-permute-start | bytes 2457608 | tf_op jit(solution)/shard_map/ppermute | solution.py:150
  152.1 8.3 %copy-start.9 = (bf16[320,1536]{1,0:T(8,128)(2,1)}, bf16[320,1536]{1,0:T(8,128)(2,1)S(1)}, u32[]{:S(2)}) copy-start(bf16[320,1536]{1,0:T(8,128)(2,1)S(1)} %collective-permute-done.12.refs_5_) | copy-start | bytes 2949124
  152.1 23.1 %collective-permute-start.30 = (bf16[5,160,512]{2,1,0:T(8,128)(2,1)}, bf16[5,160,512]{2,1,0:T(8,128)(2,1)}, u32[]{:S(2)}, u32[]{:S(2)}) collective-permute-start(bf16[5,160,512]{2,1,0:T(8,128)(2,1)} %collective-permute-done.28.refs_12_.refs_14_), channel_id=1, source_target_pairs={{0,8},{8,0},{16,24},{24,16},{1,9},{9,1},{17,25},{25,17},{2,10},{10... | collective-permute-start | bytes 2457608 | tf_op jit(solution)/shard_map/ppermute | solution.py:150
  156.7 44.5 %collective-permute-start.2 = (bf16[320,1536]{1,0:T(8,128)(2,1)S(1)}, bf16[320,1536]{1,0:T(8,128)(2,1)S(1)}, u32[]{:S(2)}, u32[]{:S(2)}) collective-permute-start(bf16[320,1536]{1,0:T(8,128)(2,1)S(1)} %collective-permute-done.refs_1_), channel_id=1, source_target_pairs={{0,2},{2,4},{4,6},{6,7},{7,5},{5,3},{3,1},{1,0},{8,10},{10,12},{12... | collective-permute-start | bytes 2949128 | tf_op jit(solution)/shard_map/ppermute | solution.py:192
  158.4 29.5 %collective-permute-start.14 = (bf16[160,1536]{1,0:T(8,128)(2,1)}, bf16[160,1536]{1,0:T(8,128)(2,1)S(1)}, u32[]{:S(2)}, u32[]{:S(2)}) collective-permute-start(bf16[160,1536]{1,0:T(8,128)(2,1)} %slice.18), channel_id=1, source_target_pairs={{0,2},{2,4},{4,6},{6,7},{7,5},{5,3},{3,1},{1,0},{8,10},{10,12},{12... | collective-permute-start | bytes 1474568 | tf_op jit(solution)/shard_map/ppermute | solution.py:192
  159.0 28.9 %collective-permute-start.15 = (bf16[160,1536]{1,0:T(8,128)(2,1)}, bf16[160,1536]{1,0:T(8,128)(2,1)S(1)}, u32[]{:S(2)}, u32[]{:S(2)}) collective-permute-start(bf16[160,1536]{1,0:T(8,128)(2,1)} %slice.19), channel_id=1, source_target_pairs={{2,0},{4,2},{6,4},{7,6},{5,7},{3,5},{1,3},{0,1},{10,8},{12,10},{14... | collective-permute-start | bytes 1474568 | tf_op jit(solution)/shard_map/ppermute | solution.py:193
  161.4 107.4 %collective-permute-start.3 = (bf16[320,1536]{1,0:T(8,128)(2,1)S(1)}, bf16[320,1536]{1,0:T(8,128)(2,1)}, u32[]{:S(2)}, u32[]{:S(2)}) collective-permute-start(bf16[320,1536]{1,0:T(8,128)(2,1)S(1)} %collective-permute-done.1.refs_2_), channel_id=1, source_target_pairs={{2,0},{4,2},{6,4},{7,6},{5,7},{3,5},{1,3},{0,1},{10,8},{12,10},{14... | collective-permute-start | bytes 2949128 | tf_op jit(solution)/shard_map/ppermute | solution.py:193
  196.3 65.1 %collective-permute-start.31 = (bf16[1,320,512]{2,1,0:T(8,128)(2,1)}, bf16[1,320,512]{2,1,0:T(8,128)(2,1)S(1)}, u32[]{:S(2)}, u32[]{:S(2)}) collective-permute-start(bf16[1,320,512]{2,1,0:T(8,128)(2,1)} %get-tuple-element.32), channel_id=1, source_target_pairs={{0,1},{1,2},{2,3},{3,4},{4,5},{5,6},{6,7},{8,9},{9,10},{10,11},{11... | collective-permute-start | bytes 983048 | tf_op jit(solution)/shard_map/ppermute | solution.py:84
  199.8 61.6 %collective-permute-start.32 = (bf16[1,320,512]{2,1,0:T(8,128)(2,1)}, bf16[1,320,512]{2,1,0:T(8,128)(2,1)S(1)}, u32[]{:S(2)}, u32[]{:S(2)}) collective-permute-start(bf16[1,320,512]{2,1,0:T(8,128)(2,1)} %get-tuple-element.33), channel_id=1, source_target_pairs={{1,0},{2,1},{3,2},{4,3},{5,4},{6,5},{7,6},{9,8},{10,9},{11,10},{12... | collective-permute-start | bytes 983048 | tf_op jit(solution)/shard_map/ppermute | solution.py:85
  201.2 94.7 %copy-start.4 = (bf16[320,1536]{1,0:T(8,128)(2,1)}, bf16[320,1536]{1,0:T(8,128)(2,1)S(1)}, u32[]{:S(2)}) copy-start(bf16[320,1536]{1,0:T(8,128)(2,1)S(1)} %collective-permute-done.2.refs_3_) | copy-start | bytes 2949124
  201.2 67.6 %collective-permute-start.4 = (bf16[320,1536]{1,0:T(8,128)(2,1)S(1)}, bf16[320,1536]{1,0:T(8,128)(2,1)}, u32[]{:S(2)}, u32[]{:S(2)}) collective-permute-start(bf16[320,1536]{1,0:T(8,128)(2,1)S(1)} %collective-permute-done.2.refs_3_), channel_id=1, source_target_pairs={{0,2},{2,4},{4,6},{6,7},{7,5},{5,3},{3,1},{1,0},{8,10},{10,12},{12... | collective-permute-start | bytes 2949128 | tf_op jit(solution)/shard_map/ppermute | solution.py:192
  203.3 26.9 %collective-permute-start.33 = (f32[2,8,128]{2,1,0:T(8,128)}, f32[2,8,128]{2,1,0:T(8,128)S(1)}, u32[]{:S(2)}, u32[]{:S(2)}) collective-permute-start(f32[2,8,128]{2,1,0:T(8,128)} %get-tuple-element.34.refs_5_), channel_id=1, source_target_pairs={{0,1},{1,0},{2,3},{3,2},{4,5},{5,4},{6,7},{7,6},{8,9},{9,8},{10,11... | collective-permute-start | bytes 24584 | tf_op jit(solution)/shard_map/ppermute | solution.py:88
  230.2 31.3 %copy-start.25 = (f32[2,8,128]{2,1,0:T(8,128)}, f32[2,8,128]{2,1,0:T(8,128)S(1)}, u32[]{:S(2)}) copy-start(f32[2,8,128]{2,1,0:T(8,128)S(1)} %collective-permute-done.33.refs_6_) | copy-start | bytes 24580
  230.2 3.9 %collective-permute-start.34 = (f32[2,8,128]{2,1,0:T(8,128)}, f32[2,8,128]{2,1,0:T(8,128)S(1)}, u32[]{:S(2)}, u32[]{:S(2)}) collective-permute-start(f32[2,8,128]{2,1,0:T(8,128)} %get-tuple-element.34.refs_5_), channel_id=1, source_target_pairs={{0,2},{1,3},{2,0},{3,1},{4,6},{5,7},{6,4},{7,5},{8,10},{9,11},{10,... | collective-permute-start | bytes 24584 | tf_op jit(solution)/shard_map/ppermute | solution.py:88
  234.0 27.4 %copy-start.27 = (f32[2,8,128]{2,1,0:T(8,128)}, f32[2,8,128]{2,1,0:T(8,128)S(1)}, u32[]{:S(2)}) copy-start(f32[2,8,128]{2,1,0:T(8,128)S(1)} %collective-permute-done.34.refs_7_) | copy-start | bytes 24580
  234.0 4.8 %collective-permute-start.35 = (f32[2,8,128]{2,1,0:T(8,128)}, f32[2,8,128]{2,1,0:T(8,128)S(1)}, u32[]{:S(2)}, u32[]{:S(2)}) collective-permute-start(f32[2,8,128]{2,1,0:T(8,128)} %get-tuple-element.34.refs_5_), channel_id=1, source_target_pairs={{0,3},{1,2},{2,1},{3,0},{4,7},{5,6},{6,5},{7,4},{8,11},{9,10},{10,... | collective-permute-start | bytes 24584 | tf_op jit(solution)/shard_map/ppermute | solution.py:88
  238.8 22.7 %copy-start.29 = (f32[2,8,128]{2,1,0:T(8,128)}, f32[2,8,128]{2,1,0:T(8,128)S(1)}, u32[]{:S(2)}) copy-start(f32[2,8,128]{2,1,0:T(8,128)S(1)} %collective-permute-done.35.refs_8_) | copy-start | bytes 24580
  238.8 4.8 %collective-permute-start.36 = (f32[2,8,128]{2,1,0:T(8,128)}, f32[2,8,128]{2,1,0:T(8,128)S(1)}, u32[]{:S(2)}, u32[]{:S(2)}) collective-permute-start(f32[2,8,128]{2,1,0:T(8,128)} %get-tuple-element.34.refs_5_), channel_id=1, source_target_pairs={{0,4},{1,5},{2,6},{3,7},{4,0},{5,1},{6,2},{7,3},{8,12},{9,13},{10,... | collective-permute-start | bytes 24584 | tf_op jit(solution)/shard_map/ppermute | solution.py:88
  243.6 17.9 %copy-start.31 = (f32[2,8,128]{2,1,0:T(8,128)}, f32[2,8,128]{2,1,0:T(8,128)S(1)}, u32[]{:S(2)}) copy-start(f32[2,8,128]{2,1,0:T(8,128)S(1)} %collective-permute-done.36.refs_9_) | copy-start | bytes 24580
  243.6 5.7 %collective-permute-start.37 = (f32[2,8,128]{2,1,0:T(8,128)}, f32[2,8,128]{2,1,0:T(8,128)S(1)}, u32[]{:S(2)}, u32[]{:S(2)}) collective-permute-start(f32[2,8,128]{2,1,0:T(8,128)} %get-tuple-element.34.refs_5_), channel_id=1, source_target_pairs={{0,5},{1,4},{2,7},{3,6},{4,1},{5,0},{6,3},{7,2},{8,13},{9,12},{10,... | collective-permute-start | bytes 24584 | tf_op jit(solution)/shard_map/ppermute | solution.py:88
  249.2 12.3 %copy-start.33 = (f32[2,8,128]{2,1,0:T(8,128)}, f32[2,8,128]{2,1,0:T(8,128)S(1)}, u32[]{:S(2)}) copy-start(f32[2,8,128]{2,1,0:T(8,128)S(1)} %collective-permute-done.37.refs_10_) | copy-start | bytes 24580
  249.2 5.7 %collective-permute-start.38 = (f32[2,8,128]{2,1,0:T(8,128)}, f32[2,8,128]{2,1,0:T(8,128)S(1)}, u32[]{:S(2)}, u32[]{:S(2)}) collective-permute-start(f32[2,8,128]{2,1,0:T(8,128)} %get-tuple-element.34.refs_5_), channel_id=1, source_target_pairs={{0,6},{1,7},{2,4},{3,5},{4,2},{5,3},{6,0},{7,1},{8,14},{9,15},{10,... | collective-permute-start | bytes 24584 | tf_op jit(solution)/shard_map/ppermute | solution.py:88
  254.9 6.6 %collective-permute-start.39 = (f32[2,8,128]{2,1,0:T(8,128)}, f32[2,8,128]{2,1,0:T(8,128)S(1)}, u32[]{:S(2)}, u32[]{:S(2)}) collective-permute-start(f32[2,8,128]{2,1,0:T(8,128)} %get-tuple-element.34.refs_5_), channel_id=1, source_target_pairs={{0,7},{1,6},{2,5},{3,4},{4,3},{5,2},{6,1},{7,0},{8,15},{9,14},{10,... | collective-permute-start | bytes 24584 | tf_op jit(solution)/shard_map/ppermute | solution.py:88
  266.7 19.3 %collective-permute-start.42 = (bf16[5,160,512]{2,1,0:T(8,128)(2,1)}, bf16[5,160,512]{2,1,0:T(8,128)(2,1)}, u32[]{:S(2)}, u32[]{:S(2)}) collective-permute-start(bf16[5,160,512]{2,1,0:T(8,128)(2,1)} %get-tuple-element.35.refs_5_.refs_7_.refs_9_), channel_id=1, source_target_pairs={{0,16},{8,24},{16,0},{24,8},{1,17},{9,25},{17,1},{25,9},{2,18},{10... | collective-permute-start | bytes 2457608 | tf_op jit(solution)/shard_map/ppermute | solution.py:150
  268.2 26.6 %collective-permute-start.43 = (bf16[5,160,512]{2,1,0:T(8,128)(2,1)}, bf16[5,160,512]{2,1,0:T(8,128)(2,1)}, u32[]{:S(2)}, u32[]{:S(2)}) collective-permute-start(bf16[5,160,512]{2,1,0:T(8,128)(2,1)} %get-tuple-element.36.refs_6_.refs_8_.refs_10_), channel_id=1, source_target_pairs={{0,16},{8,24},{16,0},{24,8},{1,17},{9,25},{17,1},{25,9},{2,18},{10... | collective-permute-start | bytes 2457608 | tf_op jit(solution)/shard_map/ppermute | solution.py:150
  268.7 27.2 %collective-permute-start.5 = (bf16[320,1536]{1,0:T(8,128)(2,1)}, bf16[320,1536]{1,0:T(8,128)(2,1)S(1)}, u32[]{:S(2)}, u32[]{:S(2)}) collective-permute-start(bf16[320,1536]{1,0:T(8,128)(2,1)} %collective-permute-done.3.refs_4_), channel_id=1, source_target_pairs={{2,0},{4,2},{6,4},{7,6},{5,7},{3,5},{1,3},{0,1},{10,8},{12,10},{14... | collective-permute-start | bytes 2949128 | tf_op jit(solution)/shard_map/ppermute | solution.py:193
  268.7 28.1 %collective-permute-start.40 = (bf16[5,160,512]{2,1,0:T(8,128)(2,1)}, bf16[5,160,512]{2,1,0:T(8,128)(2,1)S(1)}, u32[]{:S(2)}, u32[]{:S(2)}) collective-permute-start(bf16[5,160,512]{2,1,0:T(8,128)(2,1)} %get-tuple-element.35.refs_5_.refs_7_.refs_9_), channel_id=1, source_target_pairs={{0,8},{8,0},{16,24},{24,16},{1,9},{9,1},{17,25},{25,17},{2,10},{10... | collective-permute-start | bytes 2457608 | tf_op jit(solution)/shard_map/ppermute | solution.py:150
  268.8 30.1 %collective-permute-start.41 = (bf16[5,160,512]{2,1,0:T(8,128)(2,1)}, bf16[5,160,512]{2,1,0:T(8,128)(2,1)S(1)}, u32[]{:S(2)}, u32[]{:S(2)}) collective-permute-start(bf16[5,160,512]{2,1,0:T(8,128)(2,1)} %get-tuple-element.36.refs_6_.refs_8_.refs_10_), channel_id=1, source_target_pairs={{0,8},{8,0},{16,24},{24,16},{1,9},{9,1},{17,25},{25,17},{2,10},{10... | collective-permute-start | bytes 2457608 | tf_op jit(solution)/shard_map/ppermute | solution.py:150
  286.0 25.7 %collective-permute-start.44 = (bf16[5,160,512]{2,1,0:T(8,128)(2,1)}, bf16[5,160,512]{2,1,0:T(8,128)(2,1)S(1)}, u32[]{:S(2)}, u32[]{:S(2)}) collective-permute-start(bf16[5,160,512]{2,1,0:T(8,128)(2,1)} %collective-permute-done.42.refs_11_.refs_13_), channel_id=1, source_target_pairs={{0,8},{8,0},{16,24},{24,16},{1,9},{9,1},{17,25},{25,17},{2,10},{10... | collective-permute-start | bytes 2457608 | tf_op jit(solution)/shard_map/ppermute | solution.py:150
  294.8 16.9 %collective-permute-start.45 = (bf16[5,160,512]{2,1,0:T(8,128)(2,1)}, bf16[5,160,512]{2,1,0:T(8,128)(2,1)}, u32[]{:S(2)}, u32[]{:S(2)}) collective-permute-start(bf16[5,160,512]{2,1,0:T(8,128)(2,1)} %collective-permute-done.43.refs_12_.refs_14_), channel_id=1, source_target_pairs={{0,8},{8,0},{16,24},{24,16},{1,9},{9,1},{17,25},{25,17},{2,10},{10... | collective-permute-start | bytes 2457608 | tf_op jit(solution)/shard_map/ppermute | solution.py:150
  295.9 27.1 %collective-permute-start.6 = (bf16[160,1536]{1,0:T(8,128)(2,1)S(1)}, bf16[160,1536]{1,0:T(8,128)(2,1)S(1)}, u32[]{:S(2)}, u32[]{:S(2)}) collective-permute-start(bf16[160,1536]{1,0:T(8,128)(2,1)S(1)} %slice.16), channel_id=1, source_target_pairs={{0,2},{2,4},{4,6},{6,7},{7,5},{5,3},{3,1},{1,0},{8,10},{10,12},{12... | collective-permute-start | bytes 1474568 | tf_op jit(solution)/shard_map/ppermute | solution.py:192
  297.0 26.0 %collective-permute-start.7 = (bf16[160,1536]{1,0:T(8,128)(2,1)}, bf16[160,1536]{1,0:T(8,128)(2,1)S(1)}, u32[]{:S(2)}, u32[]{:S(2)}) collective-permute-start(bf16[160,1536]{1,0:T(8,128)(2,1)} %slice.17), channel_id=1, source_target_pairs={{2,0},{4,2},{6,4},{7,6},{5,7},{3,5},{1,3},{0,1},{10,8},{12,10},{14... | collective-permute-start | bytes 1474568 | tf_op jit(solution)/shard_map/ppermute | solution.py:193
  (25 other events, 48.8 us)
